TPU v7x, 256 devices: a whole 4x4x8 slice. The times are simulated.
256 devices in a mesh: ctx: 32 (over x, z), head: 8 (over y, core).
Axes of the slice: x: 4, y: 4, z: 8, core: 2. Of those that a mesh axis runs over, the one named last changes fastest.
Arguments:
- layer_input: bfloat16 [16384, 8192], P('ctx', 'head'), may hold values from -6 to 6
- query_columns: bfloat16 [16384, 8192], P('ctx', 'head'), may hold values from -6 to 6
- key_columns: bfloat16 [16384, 1024], P('ctx', 'head'), may hold values from -6 to 6
- value_columns: bfloat16 [16384, 1024], P('ctx', 'head'), may hold values from -6 to 6
- output_gradient: bfloat16 [16384, 8192], P('ctx', 'head'), may hold values from -6 to 6
Outputs:
- query_grad: bfloat16 [16384, 8192], P('ctx', 'head')
- key_weight_grad: float32 [8192, 1024], P(('head', 'ctx'))
- value_weight_grad: float32 [8192, 1024], P(('head', 'ctx'))
All inputs are finite; a program needn't handle non-finite values.
Results may differ from a plain program's by a relative error of at most 0.014.
Values may be sent and summed in bfloat16 or wider, within the bound.
A program may use at most 128 MiB of HBM per device.

v0:
```python
import jax
import jax.numpy as jnp
from jax import lax
from jax.sharding import PartitionSpec as P

QUERY_HEADS = 64
KEY_VALUE_HEADS = 8
HEAD_SIZE = 128


highest = lax.Precision.HIGHEST


def prefix(value, axis, combine, identity, reverse):
    devices, position = (lax.axis_size(axis), lax.axis_index(axis))
    everything = jax.tree.map(lambda part: lax.all_gather(part, axis), value)
    start = jax.tree.map(
        lambda part, zero: jnp.broadcast_to(jnp.asarray(zero, part.dtype), part.shape),
        value,
        identity,
    )

    def step(k, before):
        at = devices - 1 - k if reverse else k
        reached = at > position if reverse else at < position
        new = combine(before, jax.tree.map(lambda part: part[at], everything))
        return jax.tree.map(lambda a, b: jnp.where(reached, a, b), new, before)

    return lax.fori_loop(0, devices, step, start)


def positive_features(raw):
    wide = raw.astype(jnp.float32)
    return jnp.where(wide > 0, wide + 1.0, jnp.exp(jnp.minimum(wide, 0.0))).astype(jnp.bfloat16)


def feature_derivative(raw):
    wide = raw.astype(jnp.float32)
    return jnp.where(wide > 0, 1.0, jnp.exp(jnp.minimum(wide, 0.0)))


def causal_mask(length):
    rows_at = lax.broadcasted_iota(jnp.int32, (length, length), 0)
    cols_at = lax.broadcasted_iota(jnp.int32, (length, length), 1)
    return cols_at <= rows_at


def block_states(key_features, value_entries):
    states = jnp.einsum(
        "ske,skf->kef", key_features, value_entries, preferred_element_type=jnp.float32
    )
    totals = jnp.sum(key_features.astype(jnp.float32), axis=0)
    return (states, totals)


def block_scores(query_features, key_features):
    attention_scores = jnp.einsum(
        "tkge,ske->kgts", query_features, key_features, preferred_element_type=jnp.float32
    )
    return jnp.where(causal_mask(attention_scores.shape[-1]), attention_scores, jnp.float32(0.0))


def forward_blockwise_pass(
    query_features, value_entries, output_cotangent, prior_state, prior_total, attention_scores
):
    query_wide = query_features.astype(jnp.float32)
    denom = jnp.einsum("tkge,ke->tkg", query_wide, prior_total, precision=highest) + jnp.transpose(
        jnp.sum(attention_scores, axis=-1), (2, 0, 1)
    )
    numer = jnp.einsum("tkge,kef->tkgf", query_wide, prior_state, precision=highest) + jnp.einsum(
        "kgts,skf->tkgf",
        attention_scores.astype(jnp.bfloat16),
        value_entries,
        preferred_element_type=jnp.float32,
    )
    output = numer / denom[..., None]
    wide_cot = output_cotangent.astype(jnp.float32)
    scaled = (wide_cot / denom[..., None]).astype(jnp.bfloat16)
    weight = -jnp.sum(wide_cot * output, axis=-1) / denom
    grad_state = jnp.einsum(
        "tkge,tkgf->kef", query_features, scaled, preferred_element_type=jnp.float32
    )
    grad_total = jnp.einsum("tkge,tkg->ke", query_wide, weight, precision=highest)
    return (scaled, weight, grad_state, grad_total)


def backward_blockwise_pass(
    query_features,
    key_features,
    value_entries,
    lower_triangle_scores,
    scaled,
    weight,
    prior_state,
    prior_total,
    later_state,
    later_total,
):
    dscores = (
        jnp.einsum("tkgf,skf->kgts", scaled, value_entries, preferred_element_type=jnp.float32)
        + jnp.transpose(weight, (1, 2, 0))[..., None]
    )
    dscores = jnp.where(causal_mask(dscores.shape[-1]), dscores, jnp.float32(0.0)).astype(
        jnp.bfloat16
    )
    grad_query = (
        jnp.einsum("tkgf,kef->tkge", scaled.astype(jnp.float32), prior_state, precision=highest)
        + weight[..., None] * prior_total[None, :, None, :]
        + jnp.einsum("kgts,ske->tkge", dscores, key_features, preferred_element_type=jnp.float32)
    )
    key_gradient_rows = (
        jnp.einsum("kgts,tkge->ske", dscores, query_features, preferred_element_type=jnp.float32)
        + jnp.einsum(
            "kef,skf->ske", later_state, value_entries.astype(jnp.float32), precision=highest
        )
        + later_total[None]
    )
    value_gradient_rows = jnp.einsum(
        "kgts,tkgf->skf", lower_triangle_scores, scaled, preferred_element_type=jnp.float32
    ) + jnp.einsum("kef,ske->skf", later_state, key_features.astype(jnp.float32), precision=highest)
    return (grad_query, key_gradient_rows, value_gradient_rows)


def add_pair(earlier, later):
    return (earlier[0] + later[0], earlier[1] + later[1])


def shards(layer_input, query_columns, key_columns, value_columns, output_gradient):
    rows = query_columns.shape[0]
    local_kv = key_columns.shape[1] // HEAD_SIZE
    query_group_count = QUERY_HEADS // KEY_VALUE_HEADS
    block = min(256, rows)
    count = rows // block
    query_features = positive_features(query_columns).reshape(
        count, block, local_kv, query_group_count, HEAD_SIZE
    )
    key_features = positive_features(key_columns).reshape(count, block, local_kv, HEAD_SIZE)
    value_entries = value_columns.reshape(count, block, local_kv, HEAD_SIZE)
    output_cotangent = output_gradient.reshape(count, block, local_kv, query_group_count, HEAD_SIZE)
    pieces = [block_states(key_features[index], value_entries[index]) for index in range(count)]
    dev_state = pieces[0][0]
    dev_total = pieces[0][1]
    index = 1
    dev_state = dev_state + pieces[index][0]
    dev_total = dev_total + pieces[index][1]
    empty = (jnp.zeros_like(dev_state), jnp.zeros_like(dev_total))
    before_state, before_total = prefix((dev_state, dev_total), "ctx", add_pair, empty, False)
    priors = []
    running_state, running_total = (before_state, before_total)
    for index in range(count):
        priors.append((running_state, running_total))
        running_state = running_state + pieces[index][0]
        running_total = running_total + pieces[index][1]
    forwards = []
    for index in range(count):
        attention_scores = block_scores(query_features[index], key_features[index])
        forwards.append(
            forward_blockwise_pass(
                query_features[index],
                value_entries[index],
                output_cotangent[index],
                priors[index][0],
                priors[index][1],
                attention_scores,
            )
        )
    dev_gstate = forwards[0][2]
    dev_gtotal = forwards[0][3]
    index = 1
    dev_gstate = dev_gstate + forwards[index][2]
    dev_gtotal = dev_gtotal + forwards[index][3]
    after_state, after_total = prefix((dev_gstate, dev_gtotal), "ctx", add_pair, empty, True)
    laters = [None] * count
    running_state, running_total = (after_state, after_total)
    for index in range(count - 1, -1, -1):
        laters[index] = (running_state, running_total)
        running_state = running_state + forwards[index][2]
        running_total = running_total + forwards[index][3]
    query_parts = []
    key_parts = []
    value_parts = []
    for index in range(count):
        lower_triangle_scores = block_scores(query_features[index], key_features[index]).astype(
            jnp.bfloat16
        )
        grad_query, key_gradient_rows, value_gradient_rows = backward_blockwise_pass(
            query_features[index],
            key_features[index],
            value_entries[index],
            lower_triangle_scores,
            forwards[index][0],
            forwards[index][1],
            priors[index][0],
            priors[index][1],
            laters[index][0],
            laters[index][1],
        )
        query_parts.append(grad_query)
        key_parts.append(key_gradient_rows)
        value_parts.append(value_gradient_rows)
    query_grad = (
        jnp.concatenate(query_parts, axis=0).reshape(rows, query_columns.shape[1])
        * feature_derivative(query_columns)
    ).astype(jnp.bfloat16)
    key_gradient = (
        jnp.concatenate(key_parts, axis=0).reshape(rows, key_columns.shape[1])
        * feature_derivative(key_columns)
    ).astype(jnp.bfloat16)
    value_gradient = (
        jnp.concatenate(value_parts, axis=0)
        .reshape(rows, value_columns.shape[1])
        .astype(jnp.bfloat16)
    )
    key_all, value_all = (
        lax.all_gather(key_gradient, "head", axis=1, tiled=True),
        lax.all_gather(value_gradient, "head", axis=1, tiled=True),
    )
    joined = jnp.concatenate([key_all, value_all], axis=1)
    summed = lax.psum_scatter(
        jnp.einsum("tr,tc->rc", layer_input, joined, preferred_element_type=jnp.float32),
        "ctx",
        scatter_dimension=0,
        tiled=True,
    )
    half_width = key_all.shape[1]
    return (query_grad, summed[:, :half_width], summed[:, half_width:])


def solution(mesh):
    placed = (
        P("ctx", "head"),
        P("ctx", "head"),
        P("ctx", "head"),
        P("ctx", "head"),
        P("ctx", "head"),
    )
    return jax.shard_map(
        shards,
        mesh=mesh,
        in_specs=placed,
        out_specs=(P("ctx", "head"), P(("head", "ctx"), None), P(("head", "ctx"), None)),
        check_vma=False,
    )
```

profile of v0, /device:TPU:8, one launch (start us, length us, event | category | flops | bytes accessed | tf_op | source)
XLA Modules:
  0.0 587.1 jit_solution(2239093417903597590)
XLA Ops:
  9.3 1.7 convolution_add_fusion
  11.1 1.5 copy.102
  12.7 2.8 slice_convert_fusion.1
  15.5 2.5 copy.106
  18.0 1.3 copy.118
  19.4 41.8 %all-gather.5 = f32[32,1,128]{2,1,0:T(1,128)S(1)} all-gather(f32[1,1,128]{2,1,0:T(1,128)S(1)} %add_bitcast_fusion), channel_id=3, replica_groups=mesh['ctx'=32,'head'=8] {'ctx'}, dimensions={0}, use_global_device_ids=true | all-gather | bytes 16896 | tf_op jit(solution)/shard_map/all_gather | solution.py:16
  63.0 1.5 fusion.14
  64.5 27.5 %all-gather.14.cloned.1.call-done = f32[4096,128]{1,0:T(8,128)} async-done(((f32[128,128]{1,0:T(8,128)}), f32[4096,128]{1,0:T(8,128)}) %all-gather.14.cloned.1.call-update) | async-done | bytes 2097168 | tf_op jit(solution)/shard_map/all_gather | solution.py:16
  92.0 28.9 %while.34 = (s32[]{:T(128)}, f32[1,128,128]{2,1,0:T(8,128)S(1)}, f32[1,128]{1,0:T(1,128)S(1)}, s32[]{:T(128)}, f32[32,1,128,128]{3,2,1,0:T(8,128)}, /*index=5*/f32[32,1,128]{2,1,0:T(1,128)S(1)}, s32[]{:T(128)}, s32[]{:T(128)}) while((s32[]{:T(128)}, f32[1,128,128]{2,1,0:T(8,128)S(1)}, f32[1,128]{1,0:T(1,128)S(1)}, s32[]{:T(128)}, ...), condition=%wide.region_3.4_spmd.clone, body=%wide.region_2.3_spmd.clone.sunk | while | flops 49540 | bytes 198267 | solution.py:29
  120.9 2.7 fusion.105
  123.6 2.7 fusion.107
  126.3 1.5 copy.154
  127.9 1.6 copy.145
  129.5 1.4 divide_convert_fusion
  131.7 1.3 fusion.117
  134.2 2.6 convolution_bitcast_fusion.6
  136.8 1.4 convolution_bitcast_fusion.5
  139.2 2.6 copy.181
  142.8 2.6 copy.177
  145.4 2.5 fusion.30
  149.8 39.3 %all-gather.6 = f32[32,1,128]{2,1,0:T(1,128)} all-gather(f32[1,1,128]{2,1,0:T(1,128)S(1)} %fusion.41), channel_id=5, replica_groups=mesh['ctx'=32,'head'=8] {'ctx'}, dimensions={0}, use_global_device_ids=true | all-gather | bytes 16896 | tf_op jit(solution)/shard_map/all_gather | solution.py:16
  189.2 20.2 %all-gather.16.cloned.1.call-done = f32[4096,128]{1,0:T(8,128)} async-done(((f32[128,128]{1,0:T(8,128)}), f32[4096,128]{1,0:T(8,128)}) %all-gather.16.cloned.1.call-update) | async-done | bytes 2097168 | tf_op jit(solution)/shard_map/all_gather | solution.py:16
  209.4 66.8 %while.35 = (s32[]{:T(128)}, f32[1,128,128]{2,1,0:T(8,128)S(1)}, f32[1,128]{1,0:T(1,128)}, s32[]{:T(128)}, f32[32,1,128,128]{3,2,1,0:T(8,128)}, /*index=5*/f32[3...) while((s32[]{:T(128)}, f32[1,128,128]{2,1,0:T(8,128)S(1)}, f32[1,128]{1,0:T(1,128)}, ...), condition=%wide.region_9.10_spmd.clone, body=%wide.region_8.9_spmd.clone.sunk | while | flops 49544 | bytes 198329 | solution.py:29
  215.6 1.2 broadcast_select_fusion.7
  219.8 1.2 broadcast_select_fusion.7
  221.9 1.2 broadcast_select_fusion.7
  228.1 1.2 broadcast_select_fusion.7
  230.2 1.2 broadcast_select_fusion.7
  234.4 1.2 broadcast_select_fusion.7
  244.8 1.2 broadcast_select_fusion.7
  246.9 1.2 broadcast_select_fusion.7
  249.0 1.2 broadcast_select_fusion.7
  251.1 1.2 broadcast_select_fusion.7
  257.4 1.2 broadcast_select_fusion.7
  259.5 1.2 broadcast_select_fusion.7
  269.9 1.2 broadcast_select_fusion.7
  272.0 1.2 broadcast_select_fusion.7
  276.6 1.7 fusion.38
  279.9 1.6 fusion.48
  284.8 17.6 %all-gather.18.cloned.1.call-done = bf16[512,1,1024]{2,0,1:T(8,128)(2,1)} async-done(((bf16[512,1,128]{2,0,1:T(8,128)(2,1)}), bf16[512,1,1024]{2,0,1:T(8,128)(2,1)}) %all-gather.18.cloned.1.call-update) | async-done | bytes 1048592 | tf_op jit(solution)/shard_map/all_gather | solution.py:216
  302.4 29.2 %all-gather.12.cloned.1.call-done = bf16[512,1024]{1,0:T(8,128)(2,1)} async-done(((bf16[512,128]{1,0:T(8,128)(2,1)}), bf16[512,1024]{1,0:T(8,128)(2,1)}) %all-gather.12.cloned.1.call-update) | async-done | bytes 1048592 | tf_op jit(solution)/shard_map/all_gather | solution.py:215
  331.6 7.2 %convolution_bitcast_fusion = f32[1024,2048]{0,1:T(8,128)} fusion(bf16[512,1024]{1,0:T(8,128)(2,1)S(1)} %copy-done, bf16[512,1024]{1,0:T(8,128)(2,1)} %bitcast.434, bf16[512,1024]{1,0:T(8,128)(2,1)} %all-gather.12.cloned.1.call-done), kind=kOutput, calls=%fused_computation.6 | convolution fusion | flops 2151677952 | bytes 11534336 | tf_op jit(solution)/shard_map/tr,tc->rc/dot_general | solution.py:220
  338.8 9.2 %copy.191 = f32[1024,2048]{1,0:T(8,128)} copy(f32[1024,2048]{0,1:T(8,128)} %convolution_bitcast_fusion) | data formatting | bytes 16777216
  348.0 1.2 copy-done.14
  352.9 1.5 fusion.5
  354.4 2.3 copy.142
  356.6 222.3 %reduce-scatter.4.cloned.1.call-done = f32[32,2048]{1,0:T(8,128)} async-done(((f32[1024,2048]{1,0:T(8,128)}), f32[32,2048]{1,0:T(8,128)}) %reduce-scatter.4.cloned.1.call-update) | async-done | bytes 262160
  578.9 1.7 fusion.116
  (256 shorter events, 95.3 us)
Async XLA Ops:
  7.2 324.5 %copy-start = (bf16[512,1024]{1,0:T(8,128)(2,1)S(1)}, bf16[512,1024]{1,0:T(8,128)(2,1)}, u32[]{:S(2)}) copy-start(bf16[512,1024]{1,0:T(8,128)(2,1)} %param.9) | copy-start | bytes 3145732
  7.2 84.8 %all-gather.14.cloned.1.call-start = ((), (), s32[]{:S(2)}) async-start(), calls=%async_computation.2 | async-start | bytes 2162688 | tf_op jit(solution)/shard_map/all_gather | solution.py:16
  9.3 1.8 copy-start.26
  11.1 198.3 %all-gather.16.cloned.1.call-start = ((), (), s32[]{:S(2)}) async-start(), calls=%async_computation.3 | async-start | bytes 2162688 | tf_op jit(solution)/shard_map/all_gather | solution.py:16
  12.6 48.6 %copy-start.8 = (bf16[512,1024]{0,1:T(8,128)(2,1)}, bf16[512,1024]{0,1:T(8,128)(2,1)S(1)}, u32[]{:S(2)}) copy-start(bf16[512,1024]{0,1:T(8,128)(2,1)S(1)} %copy.102) | copy-start | bytes 3145732
  19.4 101.5 %copy-start.43 = (f32[128]{0:T(128)}, f32[128]{0:T(128)S(1)}, u32[]{:S(2)}) copy-start(f32[128]{0:T(128)S(1)} %get-tuple-element.360) | copy-start | bytes 1540
  61.8 0.8 copy-start.1
  61.8 1.2 copy-start.4
  64.5 64.9 %copy-start.32 = (f32[8,256]{1,0:T(8,128)}, f32[8,256]{1,0:T(8,128)S(1)}, u32[]{:S(2)}) copy-start(f32[8,256]{1,0:T(8,128)S(1)} %get-tuple-element.362) | copy-start | bytes 24580
  64.5 68.5 %copy-start.30 = (f32[8,256]{1,0:T(8,128)}, f32[8,256]{1,0:T(8,128)S(1)}, u32[]{:S(2)}) copy-start(f32[8,256]{1,0:T(8,128)S(1)} %get-tuple-element.361) | copy-start | bytes 24580
  120.9 2.7 copy-start.40
  127.9 6.2 %copy-start.34 = (f32[1,256,8]{1,2,0:T(8,128)}, f32[1,256,8]{1,2,0:T(8,128)S(1)}, u32[]{:S(2)}) copy-start(f32[1,256,8]{1,2,0:T(8,128)S(1)} %copy.154) | copy-start | bytes 24580
  129.4 4.6 copy-start.36
  129.4 3.7 copy-start.5
  129.5 3.7 copy-start.24
  130.9 0.8 copy-start.10
  133.1 12.3 %copy-start.38 = (f32[256,8]{0,1:T(8,128)}, f32[256,8]{0,1:T(8,128)S(1)}, u32[]{:S(2)}) copy-start(f32[256,8]{0,1:T(8,128)S(1)} %fusion.102) | copy-start | bytes 24580
  134.1 168.3 %all-gather.18.cloned.1.call-start = ((), (), s32[]{:S(2)}) async-start(), calls=%async_computation.4 | async-start | bytes 1179648 | tf_op jit(solution)/shard_map/all_gather | solution.py:216
  134.2 2.6 copy-start.21
  145.4 2.6 copy-start.2
  145.4 2.6 copy-start.12
  145.4 2.6 copy-start.23
  145.4 2.6 copy-start.27
  148.0 0.8 copy-start.31
  148.0 0.8 copy-start.33
  148.0 0.8 copy-start.35
  148.0 1.3 copy-start.6
  276.2 2.1 copy-start.15
  276.2 2.1 copy-start.25
  276.2 2.1 copy-start.39
  278.3 1.4 copy-start.11
  278.3 1.6 copy-start.16
  279.5 52.1 %all-gather.12.cloned.1.call-start = ((), (), s32[]{:S(2)}) async-start(), calls=%async_computation.1 | async-start | bytes 1179648 | tf_op jit(solution)/shard_map/all_gather | solution.py:215
  279.9 1.6 copy-start.22
  281.5 1.0 copy-start.17
  281.5 1.0 copy-start.19
  281.6 1.5 copy-start.42
  281.6 1.5 copy-start.46
  281.6 1.5 copy-start.7
  282.0 1.5 copy-start.13
  282.1 1.5 copy-start.3
  282.5 1.4 copy-start.29
  284.7 294.2 %reduce-scatter.4.cloned.1.call-start = ((), (), s32[]{:S(2)}) async-start(), calls=%async_computation.5 | async-start | bytes 8650752
  348.0 1.2 copy-start.14
  349.2 1.0 copy-start.20
  349.6 1.4 copy-start.18
  349.6 1.4 copy-start.28
  351.6 1.2 copy-start.9
  (4 other events, 2.7 us)
Sparse Core Ops, SparseCore 0:
  11.2 80.7 all-gather.13
  134.2 75.1 all-gather.15
  279.6 22.7 all-gather.17
  304.7 26.9 all-gather.11
  348.1 230.7 reduce-scatter.3
where the time goes:
time: 591 us; the launch traced here: 587 us
  waiting for transfers between devices  317 us (54%)
  other arithmetic  105 us (18%)
  blocking collectives  81.1 us (14%)
  matrix products  34.4 us (6%)
  local copies, waits for them, and re-layouts  33.4 us (6%)
  between operations  14.6 us (2%)
    unnamed x6, waiting for transfers between devices  222 us
    select_n x128, other arithmetic, step(): return jax.tree.map(lambda a, b: jnp.where(reached, a, b), new, before)  93.9 us
    all_gather x2, blocking collectives, prefix(): everything = jax.tree.map(lambda part: lax.all_gather(part, axis), value)  81.1 us
    all_gather x2, waiting for transfers between devices, prefix(): everything = jax.tree.map(lambda part: lax.all_gather(part, axis), value)  47.7 us
    all_gather x1, waiting for transfers between devices, shards(): lax.all_gather(key_gradient, 'head', axis=1, tiled=True)  29.2 us
    all_gather x1, waiting for transfers between devices, shards(): lax.all_gather(value_gradient, 'head', axis=1, tiled=True)  17.6 us
    unnamed x97, local copies, waits for them, and re-layouts  17.5 us
  transfers between devices with their start and end apart: 5, of which 5 were waited for; matrix products, arithmetic and copies ran while one was open for 6% of the time, Pallas kernels for 0%

commit v1 on v0

v1 whole, which is shorter than its diff:
```python
import jax
import jax.numpy as jnp
from jax import lax
from jax.experimental import pallas as pl
from jax.experimental.pallas import tpu as pltpu
from jax.sharding import PartitionSpec as P

QUERY_HEADS = 64
KEY_VALUE_HEADS = 8
GROUP = QUERY_HEADS // KEY_VALUE_HEADS
HEAD = 128
BLOCK = 256
ROWS = 512
CTX = 32
XS = 4
ZS = 8
YS = 4
PART = HEAD // CTX
MESH = pl.DeviceIdType.MESH
F32 = jnp.float32
BF16 = jnp.bfloat16
VMEM = pl.BlockSpec(memory_space=pltpu.VMEM)


def phi(raw):
    wide = raw.astype(F32)
    return jnp.where(wide > 0, wide + 1.0, jnp.exp(jnp.minimum(wide, 0.0))).astype(BF16)


def slope(raw):
    wide = raw.astype(F32)
    return jnp.where(wide > 0, 1.0, jnp.exp(jnp.minimum(wide, 0.0)))


def dot_nn(a, b):
    return lax.dot_general(a, b, (((1,), (0,)), ((), ())), preferred_element_type=F32)


def dot_nt(a, b):
    return lax.dot_general(a, b, (((1,), (1,)), ((), ())), preferred_element_type=F32)


def dot_tn(a, b):
    return lax.dot_general(a, b, (((0,), (0,)), ((), ())), preferred_element_type=F32)


def halves(value):
    high = value.astype(BF16)
    return high, (value - high.astype(F32)).astype(BF16)


def lower_mask():
    rows = lax.broadcasted_iota(jnp.int32, (BLOCK, BLOCK), 0)
    cols = lax.broadcasted_iota(jnp.int32, (BLOCK, BLOCK), 1)
    return cols <= rows


def spread_copy(source, target, send, recv, me, k):
    peer = lax.rem(me + k, CTX)
    return pltpu.make_async_remote_copy(
        src_ref=source.at[peer],
        dst_ref=target.at[me],
        send_sem=send.at[k],
        recv_sem=recv.at[k],
        device_id={"ctx": peer},
        device_id_type=MESH,
    )


def spread_start(source, target, send, recv, me):
    def one(k, carry):
        spread_copy(source, target, send, recv, me, k).start()
        return carry

    lax.fori_loop(1, CTX, one, 0)
    target[me] = source[me]


def spread_wait(source, target, send, recv, me):
    def one(k, carry):
        copy = spread_copy(source, target, send, recv, me, k)
        copy.wait_recv()
        copy.wait_send()
        return carry

    lax.fori_loop(1, CTX, one, 0)


def fill_parts(mine, state, total):
    for part in range(CTX):
        mine[part, 0:PART, :] = state[part * PART : (part + 1) * PART, :]
        mine[part, PART : 2 * PART, :] = jnp.broadcast_to(total, (PART, HEAD))


def running(inbox, outbox, reverse):
    total = jnp.zeros((2 * PART, HEAD), F32)
    for step in range(CTX):
        at = CTX - 1 - step if reverse else step
        outbox[at] = total
        total = total + inbox[at]


def join_parts(got, state):
    for part in range(CTX):
        state[part * PART : (part + 1) * PART, :] = got[part, 0:PART, :]


def greet_ctx(barrier, me):
    def one(k, carry):
        pl.semaphore_signal(
            barrier, inc=1, device_id={"ctx": lax.rem(me + k, CTX)}, device_id_type=MESH
        )
        return carry

    lax.fori_loop(1, CTX, one, 0)


def prefix_kernel(
    key, value, prior, prior_total, rows, mine, inbox, outbox, got, send_a, recv_a, send_b, recv_b
):
    me = lax.axis_index("ctx")
    barrier = pltpu.get_barrier_semaphore()
    greet_ctx(barrier, me)
    states = []
    totals = []
    for b in range(2):
        features = phi(key[b * BLOCK : (b + 1) * BLOCK, :])
        states.append(dot_tn(features, value[b * BLOCK : (b + 1) * BLOCK, :]))
        totals.append(jnp.sum(features.astype(F32), axis=0, keepdims=True))
    rows[...] = states[0] + states[1]
    fill_parts(mine, rows, totals[0] + totals[1])
    pl.semaphore_wait(barrier, CTX - 1)
    spread_start(mine, inbox, send_a, recv_a, me)
    spread_wait(mine, inbox, send_a, recv_a, me)
    running(inbox, outbox, False)
    spread_start(outbox, got, send_b, recv_b, me)
    spread_wait(outbox, got, send_b, recv_b, me)
    join_parts(got, prior.at[0])
    prior[1] = prior[0] + states[0]
    before_total = got[0, PART : PART + 1, :]
    prior_total[0] = jnp.broadcast_to(before_total, (8, HEAD))
    prior_total[1] = jnp.broadcast_to(before_total + totals[0], (8, HEAD))


def exchange_scratch():
    return [
        pltpu.VMEM((HEAD, HEAD), F32),
        pltpu.VMEM((CTX, 2 * PART, HEAD), F32),
        pltpu.VMEM((CTX, 2 * PART, HEAD), F32),
        pltpu.VMEM((CTX, 2 * PART, HEAD), F32),
        pltpu.VMEM((CTX, 2 * PART, HEAD), F32),
        pltpu.SemaphoreType.DMA((CTX,)),
        pltpu.SemaphoreType.DMA((CTX,)),
        pltpu.SemaphoreType.DMA((CTX,)),
        pltpu.SemaphoreType.DMA((CTX,)),
    ]


def attention_kernel(
    query, cotangent, key, value, prior, prior_total, query_grad, gstate, gtotal, dkey, dvalue,
    features, sums, high, low,
):
    mask = lower_mask()

    @pl.when(pl.program_id(0) == 0)
    def _():
        triangle = jnp.where(mask, 1.0, 0.0).astype(BF16)
        for b in range(2):
            at = pl.ds(b * BLOCK, BLOCK)
            kf = phi(key[at, :])
            features[at, :] = kf
            sums[at, :] = dot_nn(triangle, kf) + prior_total[b, 0:1, :]
            high[b], low[b] = halves(prior[b])
        gstate[...] = jnp.zeros_like(gstate)
        gtotal[...] = jnp.zeros_like(gtotal)
        dkey[...] = jnp.zeros_like(dkey)
        dvalue[...] = jnp.zeros_like(dvalue)

    for b in range(2):
        at = pl.ds(b * BLOCK, BLOCK)
        raw = query[at, :]
        qf = phi(raw)
        wide = qf.astype(F32)
        kf = features[at, :]
        v = value[at, :]
        scores = jnp.where(mask, dot_nt(qf, kf), 0.0).astype(BF16)
        den = jnp.sum(wide * sums[at, :], axis=1, keepdims=True)
        numer = dot_nn(qf, high[b]) + dot_nn(qf, low[b]) + dot_nn(scores, v)
        inverse = 1.0 / den
        wide_cot = cotangent[at, :].astype(F32)
        g = (wide_cot * inverse).astype(BF16)
        c = -jnp.sum(wide_cot * numer, axis=1, keepdims=True) * inverse * inverse
        gstate[b] += dot_tn(qf, g)
        gtotal[b] += jnp.broadcast_to(jnp.sum(wide * c, axis=0, keepdims=True), (8, HEAD))
        dscores = jnp.where(mask, dot_nt(g, v) + c, 0.0).astype(BF16)
        dqf = (
            dot_nt(g, high[b])
            + dot_nt(g, low[b])
            + c * prior_total[b, 0:1, :]
            + dot_nn(dscores, kf)
        )
        query_grad[at, :] = (dqf * slope(raw)).astype(BF16)
        dkey[at, :] += dot_tn(dscores, qf)
        dvalue[at, :] += dot_tn(scores, g)


def remote(source, target, send, recv, device):
    return pltpu.make_async_remote_copy(
        src_ref=source,
        dst_ref=target,
        send_sem=send,
        recv_sem=recv,
        device_id=device,
        device_id_type=MESH,
    )


def weights_kernel(
    key, value, gstate, gtotal, dkey, dvalue, layer, key_out, value_out,
    rows, mine, inbox, outbox, got, send_a, recv_a, send_b, recv_b,
    turned, gathered, zsend, zrecv, reduced, arrived,
    y_send, y_recv, f_send, f_recv, z_send, z_recv, x_send, x_recv,
):
    me = lax.axis_index("ctx")
    head = lax.axis_index("head")
    x = me // ZS
    z = lax.rem(me, ZS)
    y = head // 2
    core = lax.rem(head, 2)
    sibling = {"head": head + 1 - 2 * core}
    y_peers = [None] + [
        {"head": lax.rem(y + away, YS) * 2 + core} for away in (YS - 1, 1, 2)
    ]
    z_peers = [
        {"ctx": x * ZS + lax.rem(z + 1, ZS)},
        {"ctx": x * ZS + lax.rem(z + ZS - 1, ZS)},
    ]
    barrier = pltpu.get_barrier_semaphore()
    greet_ctx(barrier, me)
    for device in y_peers[1:] + [sibling]:
        pl.semaphore_signal(barrier, inc=1, device_id=device, device_id_type=MESH)
    rows[...] = gstate[0] + gstate[1]
    fill_parts(mine, rows, gtotal[0, 0:1, :] + gtotal[1, 0:1, :])
    zsend_zero = jnp.zeros((HEAD, 2 * HEAD), BF16)
    for wave in range(YS):
        for way in range(2):
            zrecv[wave, way, 0] = zsend_zero
    pl.semaphore_wait(barrier, CTX - 1 + YS)
    spread_start(mine, inbox, send_a, recv_a, me)
    for j in range(8):
        block = layer[:, j * HEAD : (j + 1) * HEAD].T
        for q in range(4):
            at = ((j % 2) * 4 + q) * HEAD + (j // 2) * 32
            turned[at : at + 32, :] = block[q * 32 : (q + 1) * 32, :]
    spread_wait(mine, inbox, send_a, recv_a, me)
    running(inbox, outbox, True)
    spread_start(outbox, got, send_b, recv_b, me)
    spread_wait(outbox, got, send_b, recv_b, me)
    join_parts(got, rows)
    for b in (1, 0):
        at = pl.ds(b * BLOCK, BLOCK)
        later = rows[...]
        later_total = got[0, PART : PART + 1, :]
        if b == 0:
            later = later + gstate[1]
            later_total = later_total + gtotal[1, 0:1, :]
        high, low = halves(later)
        kf = phi(key[at, :])
        v = value[at, :]
        dk = dkey[at, :] + dot_nt(v, high) + dot_nt(v, low) + later_total
        gathered[0, core, at, 0:HEAD] = (dk * slope(key[at, :])).astype(BF16)
        dv = dvalue[at, :] + dot_nn(kf, high) + dot_nn(kf, low)
        gathered[0, core, at, HEAD : 2 * HEAD] = dv.astype(BF16)

    def forward(slot):
        return remote(
            gathered.at[slot, core],
            gathered.at[slot, core],
            f_send.at[slot],
            f_recv.at[slot],
            sibling,
        )

    def forward_in(slot):
        return remote(
            gathered.at[slot, 1 - core],
            gathered.at[slot, 1 - core],
            f_send.at[slot],
            f_recv.at[slot],
            sibling,
        )

    def across(slot):
        return remote(
            gathered.at[0, core],
            gathered.at[slot, core],
            y_send.at[slot],
            y_recv.at[slot],
            y_peers[slot],
        )

    forward(0).start()
    for slot in (1, 2, 3):
        across(slot).start()

    def hop(wave, way, step):
        return remote(
            zsend.at[wave, way, step],
            zrecv.at[wave, way, step + 1],
            z_send.at[wave, way, step],
            z_recv.at[wave, way, step + 1],
            z_peers[way],
        )

    def tick(t, carry):
        for wave in range(YS):
            step = t - wave

            @pl.when(step == 0)
            def _():
                forward_in(wave).wait_recv()

            @pl.when((step >= 0) & (step < ZS))
            def _():
                for way in range(2):
                    if way == 0:
                        to = lax.rem(z + 2 * ZS - 1 - step, ZS)
                    else:
                        to = lax.rem(z + 1 + step, ZS)
                    at = pl.ds(pl.multiple_of(to * HEAD, HEAD), HEAD)
                    local = dot_nn(turned[at, :], gathered[wave, way])

                    @pl.when(step > 0)
                    def _():
                        remote(
                            zsend.at[wave, way, step - 1],
                            zrecv.at[wave, way, step],
                            z_send.at[wave, way, step - 1],
                            z_recv.at[wave, way, step],
                            z_peers[way],
                        ).wait_recv()

                    both = local + zrecv[wave, way, step].astype(F32)
                    zsend[wave, way, step] = both.astype(BF16)

                    @pl.when(step < ZS - 1)
                    def _():
                        hop(wave, way, step).start()

                    @pl.when(step == ZS - 1)
                    def _():
                        reduced[wave, way] = both

            @pl.when(step == ZS - 1)
            def _():
                for k in range(1, XS):
                    x_copy(wave, k).start()

        for slot in range(1, YS):

            @pl.when(t == slot - 1)
            def _():
                across(slot).wait_recv()
                forward(slot).start()

        return carry

    def x_copy(wave, k):
        to = lax.rem(x + k, XS)
        at = pl.ds(pl.multiple_of(to * 32, 32), 32)
        return remote(
            zsend.at[wave, :, ZS - 1, at, :],
            arrived.at[wave, k - 1],
            x_send.at[wave, k],
            x_recv.at[wave, k],
            {"ctx": to * ZS + z},
        )

    lax.fori_loop(0, ZS + YS - 1, tick, 0)
    away = [0, 1, YS - 1, 2]
    for wave in range(YS):
        for k in range(1, XS):
            x_copy(wave, k).wait_recv()
        for way in range(2):
            mine_at = pl.ds(pl.multiple_of(x * 32, 32), 32)
            total = reduced[wave, way, mine_at, :]
            for k in range(1, XS):
                total = total + arrived[wave, k - 1, way].astype(F32)
            column = (lax.rem(y + away[wave], YS) * 2 + way) * HEAD
            column = pl.ds(pl.multiple_of(column, HEAD), HEAD)
            key_out[:, column] = total[:, 0:HEAD]
            value_out[:, column] = total[:, HEAD : 2 * HEAD]
    forward(0).wait_send()
    for slot in (1, 2, 3):
        across(slot).wait_send()
        forward(slot).wait_send()

    def drain(step, carry):
        for wave in range(YS):
            for way in range(2):
                hop(wave, way, step).wait_send()
        return carry

    lax.fori_loop(0, ZS - 1, drain, 0)
    for wave in range(YS):
        for k in range(1, XS):
            x_copy(wave, k).wait_send()


def shards(layer_input, query_columns, key_columns, value_columns, output_gradient):
    shape = jax.ShapeDtypeStruct
    prior, prior_total = pl.pallas_call(
        prefix_kernel,
        out_shape=(shape((2, HEAD, HEAD), F32), shape((2, 8, HEAD), F32)),
        in_specs=[VMEM] * 2,
        out_specs=(VMEM, VMEM),
        scratch_shapes=exchange_scratch(),
        compiler_params=pltpu.CompilerParams(collective_id=0, has_side_effects=True),
        name="prefix",
    )(key_columns, value_columns)

    def whole(*dims):
        return pl.BlockSpec(dims, lambda h: (0,) * len(dims))

    column = pl.BlockSpec((ROWS, HEAD), lambda h: (0, h))
    query_grad, gstate, gtotal, dkey, dvalue = pl.pallas_call(
        attention_kernel,
        out_shape=(
            shape((ROWS, GROUP * HEAD), BF16),
            shape((2, HEAD, HEAD), F32),
            shape((2, 8, HEAD), F32),
            shape((ROWS, HEAD), F32),
            shape((ROWS, HEAD), F32),
        ),
        grid=(GROUP,),
        in_specs=[
            column,
            column,
            whole(ROWS, HEAD),
            whole(ROWS, HEAD),
            whole(2, HEAD, HEAD),
            whole(2, 8, HEAD),
        ],
        out_specs=(
            column,
            whole(2, HEAD, HEAD),
            whole(2, 8, HEAD),
            whole(ROWS, HEAD),
            whole(ROWS, HEAD),
        ),
        scratch_shapes=[
            pltpu.VMEM((ROWS, HEAD), BF16),
            pltpu.VMEM((ROWS, HEAD), F32),
            pltpu.VMEM((2, HEAD, HEAD), BF16),
            pltpu.VMEM((2, HEAD, HEAD), BF16),
        ],
        compiler_params=pltpu.CompilerParams(
            dimension_semantics=("arbitrary",), vmem_limit_bytes=24 << 20
        ),
        name="attention",
    )(query_columns, output_gradient, key_columns, value_columns, prior, prior_total)

    sems = pltpu.SemaphoreType.DMA
    key_grad, value_grad = pl.pallas_call(
        weights_kernel,
        out_shape=(
            shape((32, KEY_VALUE_HEADS * HEAD), F32),
            shape((32, KEY_VALUE_HEADS * HEAD), F32),
        ),
        in_specs=[VMEM] * 7,
        out_specs=(VMEM, VMEM),
        scratch_shapes=exchange_scratch()
        + [
            pltpu.VMEM((GROUP * HEAD, ROWS), BF16),
            pltpu.VMEM((YS, 2, ROWS, 2 * HEAD), BF16),
            pltpu.VMEM((YS, 2, ZS, HEAD, 2 * HEAD), BF16),
            pltpu.VMEM((YS, 2, ZS, HEAD, 2 * HEAD), BF16),
            pltpu.VMEM((YS, 2, HEAD, 2 * HEAD), F32),
            pltpu.VMEM((YS, XS - 1, 2, 32, 2 * HEAD), BF16),
            sems((YS,)),
            sems((YS,)),
            sems((YS,)),
            sems((YS,)),
            sems((YS, 2, ZS)),
            sems((YS, 2, ZS)),
            sems((YS, XS)),
            sems((YS, XS)),
        ],
        compiler_params=pltpu.CompilerParams(
            collective_id=1, has_side_effects=True, vmem_limit_bytes=40 << 20
        ),
        name="weights",
    )(key_columns, value_columns, gstate, gtotal, dkey, dvalue, layer_input)
    return query_grad, key_grad, value_grad


def solution(mesh):
    placed = (P("ctx", "head"),) * 5
    return jax.shard_map(
        shards,
        mesh=mesh,
        in_specs=placed,
        out_specs=(P("ctx", "head"), P(("head", "ctx"), None), P(("head", "ctx"), None)),
        check_vma=False,
    )
```

time: 591 us -> 121 us (0.20)
  waiting for transfers between devices: 317 us -> 0 us
  Pallas kernels: 0 us -> 115 us
  other arithmetic: 105 us -> 0 us
  blocking collectives: 81.1 us -> 0 us
  matrix products: 34.4 us -> 0 us
  local copies, waits for them, and re-layouts: 33.4 us -> 5.37 us
  between operations: 14.6 us -> 0.69 us
    unnamed x6 -> x0, waiting for transfers between devices: 222 us -> none
    pallas_call x0 -> x3, Pallas kernels: none -> 115 us  [the longest x1 77.2 us: shards(): pl.pallas_call(weights_kernel, out_shape=(shape((32, KEY_VALUE_HEADS * HE...]
    all_gather x4 -> x0, waiting for transfers between devices: 94.5 us -> none  [the longest x2 47.7 us: prefix(): everything = jax.tree.map(lambda part: lax.all_gather(part, axis), value)]
    select_n x128 -> x0, other arithmetic: 93.9 us -> none  [step(): return jax.tree.map(lambda a, b: jnp.where(reached, a, b), new, before)]
    all_gather x2 -> x0, blocking collectives: 81.1 us -> none  [prefix(): everything = jax.tree.map(lambda part: lax.all_gather(part, axis), value)]
    dot_general x29 -> x0, matrix products: 34.4 us -> none  [the longest x1 7.17 us: shards(): jnp.einsum('tr,tc->rc', layer_input, joined, preferred_element_type=jnp.f...]
    unnamed x97 -> x16, local copies, waits for them, and re-layouts: 17.5 us -> 5.37 us
    convert_element_type x6 -> x0, other arithmetic: 8.04 us -> none  [the longest x1 2.81 us: forward_blockwise_pass(): wide_cot = output_cotangent.astype(jnp.float32)]
  transfers between devices with their start and end apart: 5 -> 0, of which waited for: 5 -> 0; matrix products, arithmetic and copies ran while one was open for 6% -> 0% of each run, Pallas kernels for 0% -> 0%
where the time goes in v1:
time: 121 us
  Pallas kernels  115 us (95%)
  local copies, waits for them, and re-layouts  5.37 us (4%)
    pallas_call x1, Pallas kernels, shards(): pl.pallas_call(weights_kernel, out_shape=(shape((32, KEY_VALUE_HEADS * HE...  77.2 us
    pallas_call x1, Pallas kernels, shards(): pl.pallas_call(prefix_kernel, out_shape=(shape((2, HEAD, HEAD), F32), sha...  26.2 us
    pallas_call x1, Pallas kernels, shards(): pl.pallas_call(attention_kernel, out_shape=(shape((ROWS, GROUP * HEAD), B...  11.2 us
    unnamed x16, local copies, waits for them, and re-layouts  5.37 us

profile of v1, /device:TPU:8, one launch (start us, length us, event | category | flops | bytes accessed | tf_op | source)
XLA Modules:
  0.0 120.7 jit_solution(2416642934343549156)
XLA Ops:
  0.6 0.0 copy-start.1
  0.6 0.0 copy-start
  0.7 26.2 %prefix.1 = (f32[2,128,128]{2,1,0:T(8,128)}, f32[2,8,128]{2,1,0:T(8,128)}) custom-call(bf16[512,128]{1,0:T(8,128)(2,1)} %key.5, bf16[512,128]{1,0:T(8,128)(2,1)} %value.5), custom_call_target="tpu_custom_call" | custom-call | tf_op jit(solution)/shard_map/prefix/pallas_call | solution.py:412
  26.9 0.0 copy-done.1
  26.9 0.0 copy-done
  26.9 0.0 copy-start.2
  26.9 1.2 %copy-done.2 = bf16[512,1024]{1,0:T(8,128)(2,1)S(1)} copy-done((bf16[512,1024]{1,0:T(8,128)(2,1)S(1)}, bf16[512,1024]{1,0:T(8,128)(2,1)}, u32[]{:S(2)}) %copy-start.2) | copy-done | bytes 1048600
  28.2 0.0 copy-start.3
  28.2 1.2 %copy-done.3 = bf16[512,1024]{1,0:T(8,128)(2,1)S(1)} copy-done((bf16[512,1024]{1,0:T(8,128)(2,1)S(1)}, bf16[512,1024]{1,0:T(8,128)(2,1)}, u32[]{:S(2)}) %copy-start.3) | copy-done | bytes 1048600
  29.4 0.0 copy-start.5
  29.4 0.9 copy-done.5
  30.3 0.0 copy-start.6
  30.3 0.7 copy-done.6
  31.0 0.0 copy-start.4
  31.0 11.2 %attention.1 = (bf16[512,1024]{1,0:T(8,128)(2,1)}, f32[2,128,128]{2,1,0:T(8,128)S(1)}, f32[2,8,128]{2,1,0:T(8,128)S(1)}, f32[512,128]{1,0:T(8,128)S(1)}, f32[512,128]{1,0:T(8,128)S(1)}) custom-call(bf16[512,1024]{1,0:T(8,128)(2,1)S(1)} %copy-done.2, bf16[512,1024]{1,0:T(8,128)(2,1)S(1)} %copy-done.3, bf16[512,128]{1,0:T(8,128)(2,1)S(1)} %copy-done, ...), custom_call_target="tpu_custom_call" | custom-call | tf_op jit(solution)/shard_map/attention/pallas_call | solution.py:426
  42.2 0.0 copy-done.4
  42.2 77.2 %weights.1 = (f32[32,1024]{1,0:T(8,128)S(1)}, f32[32,1024]{1,0:T(8,128)S(1)}) custom-call(bf16[512,128]{1,0:T(8,128)(2,1)S(1)} %copy-done, bf16[512,128]{1,0:T(8,128)(2,1)S(1)} %copy-done.1, f32[2,128,128]{2,1,0:T(8,128)S(1)} %get-tuple-element.15.gstate, f32[2,8,128]{2,1,0:T(8,128)S(1)} %get-tuple-element.16.gtotal, f32[512,128]{1,0:T(8,128)S(1)} %get-tuple-element.17.dkey, ...), custom_call_target="tpu_custom_call" | custom-call | tf_op jit(solution)/shard_map/weights/pallas_call | solution.py:464
  119.4 0.7 copy.10
  120.0 0.7 copy.11
Async XLA Ops:
  0.6 26.3 %copy-start.1 = (bf16[512,128]{1,0:T(8,128)(2,1)S(1)}, bf16[512,128]{1,0:T(8,128)(2,1)}, u32[]{:S(2)}) copy-start(bf16[512,128]{1,0:T(8,128)(2,1)} %value.5) | copy-start | bytes 393220
  0.6 26.3 %copy-start = (bf16[512,128]{1,0:T(8,128)(2,1)S(1)}, bf16[512,128]{1,0:T(8,128)(2,1)}, u32[]{:S(2)}) copy-start(bf16[512,128]{1,0:T(8,128)(2,1)} %key.5) | copy-start | bytes 393220
  26.9 1.2 %copy-start.2 = (bf16[512,1024]{1,0:T(8,128)(2,1)S(1)}, bf16[512,1024]{1,0:T(8,128)(2,1)}, u32[]{:S(2)}) copy-start(bf16[512,1024]{1,0:T(8,128)(2,1)} %query.1) | copy-start | bytes 3145732
  28.2 1.2 %copy-start.3 = (bf16[512,1024]{1,0:T(8,128)(2,1)S(1)}, bf16[512,1024]{1,0:T(8,128)(2,1)}, u32[]{:S(2)}) copy-start(bf16[512,1024]{1,0:T(8,128)(2,1)} %cotangent.1) | copy-start | bytes 3145732
  29.4 0.9 copy-start.5
  30.3 0.7 copy-start.6
  31.0 11.2 %copy-start.4 = (bf16[512,1024]{1,0:T(8,128)(2,1)S(1)}, bf16[512,1024]{1,0:T(8,128)(2,1)}, u32[]{:S(2)}) copy-start(bf16[512,1024]{1,0:T(8,128)(2,1)} %layer.1) | copy-start | bytes 3145732

commit v2 on v1

v2 whole, which is shorter than its diff:
```python
import jax
import jax.numpy as jnp
from jax import lax
from jax.experimental import pallas as pl
from jax.experimental.pallas import tpu as pltpu
from jax.sharding import PartitionSpec as P

QUERY_HEADS = 64
KEY_VALUE_HEADS = 8
GROUP = QUERY_HEADS // KEY_VALUE_HEADS
HEAD = 128
BLOCK = 256
ROWS = 512
XS = 4
ZS = 8
YS = 4
OUT = 32
MESSAGE = HEAD + 16
MESH = pl.DeviceIdType.MESH
F32 = jnp.float32
BF16 = jnp.bfloat16
HOPS = ((4, 3), (3, 4))
LAST = 4


def phi(raw):
    wide = raw.astype(F32)
    return jnp.where(wide > 0, wide + 1.0, jnp.exp(jnp.minimum(wide, 0.0))).astype(BF16)


def slope(raw):
    wide = raw.astype(F32)
    return jnp.where(wide > 0, 1.0, jnp.exp(jnp.minimum(wide, 0.0)))


def dot_nn(a, b):
    return lax.dot_general(a, b, (((1,), (0,)), ((), ())), preferred_element_type=F32)


def dot_nt(a, b):
    return lax.dot_general(a, b, (((1,), (1,)), ((), ())), preferred_element_type=F32)


def dot_tn(a, b):
    return lax.dot_general(a, b, (((0,), (0,)), ((), ())), preferred_element_type=F32)


def halves(value):
    high = value.astype(BF16)
    return high, (value - high.astype(F32)).astype(BF16)


def lower_mask():
    rows = lax.broadcasted_iota(jnp.int32, (BLOCK, BLOCK), 0)
    cols = lax.broadcasted_iota(jnp.int32, (BLOCK, BLOCK), 1)
    return cols <= rows


def remote(source, target, send, recv, device):
    return pltpu.make_async_remote_copy(
        src_ref=source,
        dst_ref=target,
        send_sem=send,
        recv_sem=recv,
        device_id=device,
        device_id_type=MESH,
    )


def pack(target, state, total):
    target[0:HEAD, :] = state.astype(BF16)
    high, low = halves(total)
    row = lax.broadcasted_iota(jnp.int32, (16, HEAD), 0)
    tail = jnp.where(row == 0, high.astype(F32), jnp.where(row == 1, low.astype(F32), 0.0))
    target[HEAD:MESSAGE, :] = tail.astype(BF16)


def parts(message):
    return message[0:HEAD, :], message[HEAD : HEAD + 1, :] + message[HEAD + 1 : HEAD + 2, :]


def kernel(
    query_hbm, cotangent_hbm, key_hbm, value_hbm, layer_hbm,
    query_grad_hbm, key_out, value_out,
    query, cotangent, key, value, layer,
    features, sums, states, totals, high, low, prior_total, rowsum,
    qf_all, scores_all, numer_all, g_all, c_all, grad_all,
    gstate, gtotal, dkey, dvalue,
    message, from_z, from_x,
    turned, gathered, zsend, zrecv, reduced, reduced_low, arrived,
    load, zs, zr, xs, xr, y_send, y_recv, f_send, f_recv, p_send, p_recv, x_send, x_recv,
):
    me = lax.axis_index("ctx")
    head = lax.axis_index("head")
    x = me // ZS
    z = lax.rem(me, ZS)
    y = head // 2
    core = lax.rem(head, 2)
    sibling = {"head": head + 1 - 2 * core}
    z_line = [{"ctx": x * ZS + lax.rem(z + k, ZS)} for k in range(ZS)]
    x_line = [{"ctx": lax.rem(x + k, XS) * ZS + z} for k in range(XS)]
    y_line = [{"head": lax.rem(y + k, YS) * 2 + core} for k in (0, YS - 1, 1, 2)]
    away = (0, 1, YS - 1, 2)

    loads = [
        pltpu.make_async_copy(source, target, load.at[i])
        for i, (source, target) in enumerate(
            (
                (key_hbm, key),
                (value_hbm, value),
                (query_hbm, query),
                (cotangent_hbm, cotangent),
                (layer_hbm, layer),
            )
        )
    ]
    for copy in loads:
        copy.start()
    barrier = pltpu.get_barrier_semaphore()
    for device in z_line[1:] + x_line[1:] + y_line[1:] + [sibling]:
        pl.semaphore_signal(barrier, inc=1, device_id=device, device_id_type=MESH)

    def z_copy(e, k):
        return remote(message.at[e, 0], from_z.at[e, k], zs.at[e, k], zr.at[e, k], z_line[k])

    def x_copy(e, k):
        return remote(message.at[e, 1], from_x.at[e, k], xs.at[e, k], xr.at[e, k], x_line[k])

    def z_finish(e, state, total, reverse):
        line_state, line_total = state, total
        part_state, part_total = jnp.zeros_like(state), jnp.zeros_like(total)
        for k in range(1, ZS):
            z_copy(e, k).wait_recv()
            got_state, got_total = parts(from_z[e, k].astype(F32))
            line_state, line_total = line_state + got_state, line_total + got_total
            counts = (k > z) if reverse else (k <= z)
            part_state = part_state + jnp.where(counts, got_state, 0.0)
            part_total = part_total + jnp.where(counts, got_total, 0.0)
        pack(message.at[e, 1], line_state, line_total)
        for k in range(1, XS):
            x_copy(e, k).start()
        rowsum[0:HEAD, :] = part_state
        rowsum[HEAD : HEAD + 8, :] = jnp.broadcast_to(part_total, (8, HEAD))

    def x_finish(e, reverse):
        state, total = rowsum[0:HEAD, :], rowsum[HEAD : HEAD + 1, :]
        for k in range(1, XS):
            x_copy(e, k).wait_recv()
            got_state, got_total = parts(from_x[e, k].astype(F32))
            counts = (k > x) if reverse else (k <= x)
            state = state + jnp.where(counts, got_state, 0.0)
            total = total + jnp.where(counts, got_total, 0.0)
        return state, total

    mask = lower_mask()
    blocks = [pl.ds(b * BLOCK, BLOCK) for b in range(2)]

    loads[0].wait()
    loads[1].wait()
    for b in range(2):
        kf = phi(key[blocks[b], :])
        features[blocks[b], :] = kf
        states[b] = dot_tn(kf, value[blocks[b], :])
        totals[b] = jnp.broadcast_to(
            jnp.sum(kf.astype(F32), axis=0, keepdims=True), (8, HEAD)
        )
    own_total = totals[0, 0:1, :] + totals[1, 0:1, :]
    pack(message.at[0, 0], states[0] + states[1], own_total)
    pl.semaphore_wait(barrier, ZS - 1 + XS - 1 + YS - 1 + 1)
    for k in range(1, ZS):
        z_copy(0, k).start()

    triangle = jnp.where(mask, 1.0, 0.0).astype(BF16)
    for b in range(2):
        sums[blocks[b], :] = dot_nn(triangle, features[blocks[b], :])
    zero = jnp.zeros((HEAD, 2 * HEAD), BF16)
    for wave in range(YS):
        for way in range(2):
            for side in range(2):
                zrecv[wave, way, side, 0] = zero
    gstate[...] = jnp.zeros_like(gstate)
    gtotal[...] = jnp.zeros_like(gtotal)
    dkey[...] = jnp.zeros_like(dkey)
    dvalue[...] = jnp.zeros_like(dvalue)

    def columns(h):
        return pl.ds(pl.multiple_of(h * HEAD, HEAD), HEAD)

    def inside(h, carry):
        at = columns(h)
        for b in range(2):
            qf = phi(query[blocks[b], at])
            qf_all[blocks[b], at] = qf
            scores = jnp.where(mask, dot_nt(qf, features[blocks[b], :]), 0.0).astype(BF16)
            scores_all[h, b] = scores
            numer_all[blocks[b], at] = dot_nn(scores, value[blocks[b], :])
        return carry

    def forward_pass(h, carry):
        at = columns(h)
        for b in range(2):
            qf = qf_all[blocks[b], at]
            wide = qf.astype(F32)
            den = jnp.sum(wide * sums[blocks[b], :], axis=1, keepdims=True)
            numer = numer_all[blocks[b], at] + dot_nn(qf, high[b]) + dot_nn(qf, low[b])
            inverse = 1.0 / den
            wide_cot = cotangent[blocks[b], at].astype(F32)
            g = (wide_cot * inverse).astype(BF16)
            c = -jnp.sum(wide_cot * numer, axis=1, keepdims=True) * inverse * inverse
            c = jnp.broadcast_to(c, (BLOCK, HEAD))
            g_all[blocks[b], at] = g
            c_all[blocks[b], at] = c
            gstate[b] += dot_tn(qf, g)
            gtotal[b] += jnp.broadcast_to(jnp.sum(wide * c, axis=0, keepdims=True), (8, HEAD))
        return carry

    def backward_pass(h, carry):
        at = columns(h)
        for b in range(2):
            g = g_all[blocks[b], at]
            qf = qf_all[blocks[b], at]
            c = c_all[blocks[b], at]
            kf = features[blocks[b], :]
            dscores = dot_nt(g, value[blocks[b], :]) + jnp.concatenate([c, c], axis=1)
            dscores = jnp.where(mask, dscores, 0.0).astype(BF16)
            dqf = (
                dot_nt(g, high[b])
                + dot_nt(g, low[b])
                + c * prior_total[b, 0:1, :]
                + dot_nn(dscores, kf)
            )
            grad_all[blocks[b], at] = (dqf * slope(query[blocks[b], at])).astype(BF16)
            dkey[blocks[b], :] += dot_tn(dscores, qf)
            dvalue[blocks[b], :] += dot_tn(scores_all[h, b], g)
        return carry

    loads[2].wait()
    lax.fori_loop(0, GROUP // 2, inside, 0)
    z_finish(0, states[0] + states[1], own_total, False)
    lax.fori_loop(GROUP // 2, GROUP, inside, 0)
    loads[3].wait()
    state, total = x_finish(0, False)
    for b in range(2):
        high[b], low[b] = halves(state)
        prior_total[b] = jnp.broadcast_to(total, (8, HEAD))
        sums[blocks[b], :] += total
        state = state + states[b]
        total = total + totals[b, 0:1, :]
    lax.fori_loop(0, GROUP, forward_pass, 0)
    own_gtotal = gtotal[0, 0:1, :] + gtotal[1, 0:1, :]
    pack(message.at[1, 0], gstate[0] + gstate[1], own_gtotal)
    for k in range(1, ZS):
        z_copy(1, k).start()
    lax.fori_loop(0, GROUP // 2, backward_pass, 0)
    z_finish(1, gstate[0] + gstate[1], own_gtotal, True)
    lax.fori_loop(GROUP // 2, GROUP, backward_pass, 0)
    grad_copy = pltpu.make_async_copy(grad_all, query_grad_hbm, load.at[5])
    grad_copy.start()
    loads[4].wait()
    for j in range(8):
        block = layer[:, j * HEAD : (j + 1) * HEAD].T
        for q in range(4):
            turned[(j % 2) * 4 + q, j // 2] = block[q * OUT : (q + 1) * OUT, :]
    later, later_total = x_finish(1, True)
    for b in (1, 0):
        later_high, later_low = halves(later)
        v = value[blocks[b], :]
        kf = features[blocks[b], :]
        dk = dkey[blocks[b], :] + dot_nt(v, later_high) + dot_nt(v, later_low) + later_total
        gathered[0, core, blocks[b], 0:HEAD] = (dk * slope(key[blocks[b], :])).astype(BF16)
        dv = dvalue[blocks[b], :] + dot_nn(kf, later_high) + dot_nn(kf, later_low)
        gathered[0, core, blocks[b], HEAD : 2 * HEAD] = dv.astype(BF16)
        later = later + gstate[b]
        later_total = later_total + gtotal[b, 0:1, :]

    def forward(slot):
        return remote(
            gathered.at[slot, core],
            gathered.at[slot, core],
            f_send.at[slot],
            f_recv.at[slot],
            sibling,
        )

    def forward_in(slot):
        return remote(
            gathered.at[slot, 1 - core],
            gathered.at[slot, 1 - core],
            f_send.at[slot],
            f_recv.at[slot],
            sibling,
        )

    def across(slot):
        return remote(
            gathered.at[0, core],
            gathered.at[slot, core],
            y_send.at[slot],
            y_recv.at[slot],
            y_line[slot],
        )

    forward(0).start()
    for slot in (1, 2, 3):
        across(slot).start()

    def hop(wave, way, side, step):
        return remote(
            zsend.at[wave, way, side, step],
            zrecv.at[wave, way, side, step + 1],
            p_send.at[wave, way, side, step],
            p_recv.at[wave, way, side, step + 1],
            z_line[1 if side == 0 else ZS - 1],
        )

    def owed(wave, k):
        to = lax.rem(x + k, XS)
        at = pl.ds(pl.multiple_of(to * OUT, OUT), OUT)
        return remote(
            reduced_low.at[wave, :, at, :],
            arrived.at[wave, k],
            x_send.at[wave, k],
            x_recv.at[wave, k],
            x_line[k],
        )

    def local(wave, way, to):
        rows = turned[to].reshape(HEAD, ROWS)
        return dot_nn(rows, gathered[wave, way])

    def tick(i, carry):
        wave = lax.rem(i, YS)
        step = i // YS - wave

        for slot in range(1, YS):

            @pl.when((step == -1) & (wave == slot))
            def _():
                across(slot).wait_recv()
                forward(slot).start()

        @pl.when(step == 0)
        def _():
            forward_in(wave).wait_recv()

        for way in range(2):
            for side in range(2):
                hops = HOPS[way][side]

                @pl.when((step >= 0) & (step < hops))
                def _():
                    left = hops - step
                    to = lax.rem(z + left, ZS) if side == 0 else lax.rem(z + ZS - left, ZS)
                    mine = local(wave, way, to)

                    @pl.when(step > 0)
                    def _():
                        hop(wave, way, side, step - 1).wait_recv()

                    both = mine + zrecv[wave, way, side, step].astype(F32)
                    zsend[wave, way, side, step] = both.astype(BF16)
                    hop(wave, way, side, step).start()

        @pl.when(step == LAST)
        def _():
            for way in range(2):
                total = local(wave, way, z)
                for side in range(2):
                    hops = HOPS[way][side]
                    hop(wave, way, side, hops - 1).wait_recv()
                    total = total + zrecv[wave, way, side, hops].astype(F32)
                reduced[wave, way] = total
                reduced_low[wave, way] = total.astype(BF16)
            for k in range(1, XS):
                owed(wave, k).start()

        return carry

    lax.fori_loop(0, YS * (LAST + YS), tick, 0)
    mine_at = pl.ds(pl.multiple_of(x * OUT, OUT), OUT)
    for wave in range(YS):
        for k in range(1, XS):
            owed(wave, k).wait_recv()
        for way in range(2):
            total = reduced[wave, way, mine_at, :]
            for k in range(1, XS):
                total = total + arrived[wave, k, way].astype(F32)
            column = columns(lax.rem(y + away[wave], YS) * 2 + way)
            key_out[:, column] = total[:, 0:HEAD]
            value_out[:, column] = total[:, HEAD : 2 * HEAD]

    for e in range(2):
        for k in range(1, ZS):
            z_copy(e, k).wait_send()
        for k in range(1, XS):
            x_copy(e, k).wait_send()
    forward(0).wait_send()
    for slot in (1, 2, 3):
        across(slot).wait_send()
        forward(slot).wait_send()

    def drain(wave, carry):
        for way in range(2):
            for side in range(2):
                for step in range(HOPS[way][side]):
                    hop(wave, way, side, step).wait_send()
        for k in range(1, XS):
            owed(wave, k).wait_send()
        return carry

    lax.fori_loop(0, YS, drain, 0)
    grad_copy.wait()


def shards(layer_input, query_columns, key_columns, value_columns, output_gradient):
    shape = jax.ShapeDtypeStruct
    vmem = pltpu.VMEM
    sems = pltpu.SemaphoreType.DMA
    wide = GROUP * HEAD
    far = pl.BlockSpec(memory_space=pl.ANY)
    near = pl.BlockSpec(memory_space=pltpu.VMEM)
    return pl.pallas_call(
        kernel,
        out_shape=(
            shape((ROWS, wide), BF16),
            shape((OUT, KEY_VALUE_HEADS * HEAD), F32),
            shape((OUT, KEY_VALUE_HEADS * HEAD), F32),
        ),
        in_specs=[far] * 5,
        out_specs=(far, near, near),
        scratch_shapes=[
            vmem((ROWS, wide), BF16),
            vmem((ROWS, wide), BF16),
            vmem((ROWS, HEAD), BF16),
            vmem((ROWS, HEAD), BF16),
            vmem((ROWS, wide), BF16),
            vmem((ROWS, HEAD), BF16),
            vmem((ROWS, HEAD), F32),
            vmem((2, HEAD, HEAD), F32),
            vmem((2, 8, HEAD), F32),
            vmem((2, HEAD, HEAD), BF16),
            vmem((2, HEAD, HEAD), BF16),
            vmem((2, 8, HEAD), F32),
            vmem((HEAD + 8, HEAD), F32),
            vmem((ROWS, wide), BF16),
            vmem((GROUP, 2, BLOCK, BLOCK), BF16),
            vmem((ROWS, wide), F32),
            vmem((ROWS, wide), BF16),
            vmem((ROWS, wide), F32),
            vmem((ROWS, wide), BF16),
            vmem((2, HEAD, HEAD), F32),
            vmem((2, 8, HEAD), F32),
            vmem((ROWS, HEAD), F32),
            vmem((ROWS, HEAD), F32),
            vmem((2, 2, MESSAGE, HEAD), BF16),
            vmem((2, ZS, MESSAGE, HEAD), BF16),
            vmem((2, XS, MESSAGE, HEAD), BF16),
            vmem((ZS, XS, OUT, ROWS), BF16),
            vmem((YS, 2, ROWS, 2 * HEAD), BF16),
            vmem((YS, 2, 2, LAST, HEAD, 2 * HEAD), BF16),
            vmem((YS, 2, 2, LAST + 1, HEAD, 2 * HEAD), BF16),
            vmem((YS, 2, HEAD, 2 * HEAD), F32),
            vmem((YS, 2, HEAD, 2 * HEAD), BF16),
            vmem((YS, XS, 2, OUT, 2 * HEAD), BF16),
            sems((6,)),
            sems((2, ZS)),
            sems((2, ZS)),
            sems((2, XS)),
            sems((2, XS)),
            sems((YS,)),
            sems((YS,)),
            sems((YS,)),
            sems((YS,)),
            sems((YS, 2, 2, LAST)),
            sems((YS, 2, 2, LAST + 1)),
            sems((YS, XS)),
            sems((YS, XS)),
        ],
        compiler_params=pltpu.CompilerParams(
            collective_id=0, has_side_effects=True, vmem_limit_bytes=48 << 20
        ),
        name="backward",
    )(query_columns, output_gradient, key_columns, value_columns, layer_input)


def solution(mesh):
    placed = (P("ctx", "head"),) * 5
    return jax.shard_map(
        shards,
        mesh=mesh,
        in_specs=placed,
        out_specs=(P("ctx", "head"), P(("head", "ctx"), None), P(("head", "ctx"), None)),
        check_vma=False,
    )
```

time: 121 us -> 102 us (0.84)
  Pallas kernels: 115 us -> 92.3 us
  local copies, waits for them, and re-layouts: 5.37 us -> 7.76 us
    pallas_call x3 -> x1, Pallas kernels: 115 us -> 92.3 us  [shards(): pl.pallas_call(kernel, out_shape=(shape((ROWS, wide), BF16), shape((OUT,...]
    unnamed x16 -> x13, local copies, waits for them, and re-layouts: 5.37 us -> 7.76 us
where the time goes in v2:
time: 102 us; the launch traced here: 101 us
  Pallas kernels  92.3 us (90%)
  local copies, waits for them, and re-layouts  7.76 us (8%)
    pallas_call x1, Pallas kernels, shards(): pl.pallas_call(kernel, out_shape=(shape((ROWS, wide), BF16), shape((OUT,...  92.3 us
    unnamed x13, local copies, waits for them, and re-layouts  7.76 us

profile of v2, /device:TPU:8, one launch (start us, length us, event | category | flops | bytes accessed | tf_op | source)
XLA Modules:
  0.0 100.7 jit_solution(15753246217596847759)
XLA Ops:
  0.6 0.0 copy-start
  0.6 1.2 %copy-done = bf16[512,1024]{1,0:T(8,128)(2,1)S(1)} copy-done((bf16[512,1024]{1,0:T(8,128)(2,1)S(1)}, bf16[512,1024]{1,0:T(8,128)(2,1)}, u32[]{:S(2)}) %copy-start) | copy-done | bytes 1048600
  1.9 0.0 copy-start.1
  1.9 1.2 %copy-done.1 = bf16[512,1024]{1,0:T(8,128)(2,1)S(1)} copy-done((bf16[512,1024]{1,0:T(8,128)(2,1)S(1)}, bf16[512,1024]{1,0:T(8,128)(2,1)}, u32[]{:S(2)}) %copy-start.1) | copy-done | bytes 1048600
  3.1 0.0 copy-start.2
  3.1 1.2 %copy-done.2 = bf16[512,1024]{1,0:T(8,128)(2,1)S(1)} copy-done((bf16[512,1024]{1,0:T(8,128)(2,1)S(1)}, bf16[512,1024]{1,0:T(8,128)(2,1)}, u32[]{:S(2)}) %copy-start.2) | copy-done | bytes 1048600
  4.3 0.0 copy-start.3
  4.3 0.9 copy-done.3
  5.2 0.0 copy-start.4
  5.2 0.9 copy-done.4
  6.1 92.3 %backward.1 = (bf16[512,1024]{1,0:T(8,128)(2,1)S(1)}, f32[32,1024]{1,0:T(8,128)S(1)}, f32[32,1024]{1,0:T(8,128)S(1)}) custom-call(bf16[512,1024]{1,0:T(8,128)(2,1)S(1)} %copy-done, bf16[512,1024]{1,0:T(8,128)(2,1)S(1)} %copy-done.1, bf16[512,128]{1,0:T(8,128)(2,1)S(1)} %copy-done.3, bf16[512,128]{1,0:T(8,128)(2,1)S(1)} %copy-done.4, ...), custom_call_target="tpu_custom_call" | custom-call | tf_op jit(solution)/shard_map/backward/pallas_call | solution.py:422
  98.4 1.0 copy.11
  99.4 0.7 copy.12
  100.1 0.7 copy.13
Async XLA Ops:
  0.6 1.2 %copy-start = (bf16[512,1024]{1,0:T(8,128)(2,1)S(1)}, bf16[512,1024]{1,0:T(8,128)(2,1)}, u32[]{:S(2)}) copy-start(bf16[512,1024]{1,0:T(8,128)(2,1)} %query_hbm.1) | copy-start | bytes 3145732
  1.9 1.2 %copy-start.1 = (bf16[512,1024]{1,0:T(8,128)(2,1)S(1)}, bf16[512,1024]{1,0:T(8,128)(2,1)}, u32[]{:S(2)}) copy-start(bf16[512,1024]{1,0:T(8,128)(2,1)} %cotangent_hbm.1) | copy-start | bytes 3145732
  3.1 1.2 %copy-start.2 = (bf16[512,1024]{1,0:T(8,128)(2,1)S(1)}, bf16[512,1024]{1,0:T(8,128)(2,1)}, u32[]{:S(2)}) copy-start(bf16[512,1024]{1,0:T(8,128)(2,1)} %layer_hbm.1) | copy-start | bytes 3145732
  4.3 0.9 copy-start.3
  5.2 0.9 copy-start.4

commit v3 on v2

--- a/solution.py
+++ b/solution.py
@@ -19,8 +19,12 @@
 MESH = pl.DeviceIdType.MESH
 F32 = jnp.float32
 BF16 = jnp.bfloat16
-HOPS = ((4, 3), (3, 4))
-LAST = 4
+HALF = 512
+LONG = 4
+SHORT = 3
+ZFIRST = 3
+XFIRST = 5
+LIMIT = 60 << 20
 
 
 def phi(raw):
@@ -87,8 +91,9 @@
     qf_all, scores_all, numer_all, g_all, c_all, grad_all,
     gstate, gtotal, dkey, dvalue,
     message, from_z, from_x,
-    turned, gathered, zsend, zrecv, reduced, reduced_low, arrived,
-    load, zs, zr, xs, xr, y_send, y_recv, f_send, f_recv, p_send, p_recv, x_send, x_recv,
+    turned, paired, zsend, zrecv, xsend, xrecv, x_owed, z_owed, x_arrived, z_arrived,
+    load, zs, zr, xs, xr, l_send, l_recv, f_send, f_recv,
+    p_send, p_recv, q_send, q_recv, x_send, x_recv, z_send, z_recv,
 ):
     me = lax.axis_index("ctx")
     head = lax.axis_index("head")
@@ -99,8 +104,7 @@
     sibling = {"head": head + 1 - 2 * core}
     z_line = [{"ctx": x * ZS + lax.rem(z + k, ZS)} for k in range(ZS)]
     x_line = [{"ctx": lax.rem(x + k, XS) * ZS + z} for k in range(XS)]
-    y_line = [{"head": lax.rem(y + k, YS) * 2 + core} for k in (0, YS - 1, 1, 2)]
-    away = (0, 1, YS - 1, 2)
+    y_line = [{"head": lax.rem(y + k, YS) * 2 + core} for k in range(YS)]
 
     loads = [
         pltpu.make_async_copy(source, target, load.at[i])
@@ -110,7 +114,7 @@
                 (value_hbm, value),
                 (query_hbm, query),
                 (cotangent_hbm, cotangent),
-                (layer_hbm, layer),
+                (layer_hbm, layer.at[0]),
             )
         )
     ]
@@ -170,14 +174,47 @@
     for k in range(1, ZS):
         z_copy(0, k).start()
 
+    def layer_copy(slot, half):
+        part = pl.ds(half * HALF, HALF)
+        return remote(
+            layer.at[0, :, part],
+            layer.at[slot, :, part],
+            l_send.at[slot, half],
+            l_recv.at[slot, half],
+            y_line[YS - 1 if slot == 1 else 1],
+        )
+
+    def layer_relay(half):
+        part = pl.ds(half * HALF, HALF)
+        return remote(
+            layer.at[1 + core, :, part],
+            layer.at[3, :, part],
+            l_send.at[3, half],
+            l_recv.at[3, half],
+            {"head": lax.rem(y + YS - 1 + 2 * core, YS) * 2 + core},
+        )
+
+    def turn(slot, half):
+        def one(i, carry):
+            j = half * 4 + i
+            block = layer[slot, :, pl.ds(pl.multiple_of(j * HEAD, HEAD), HEAD)].T
+            for q in range(4):
+                turned[slot, lax.rem(j, 2) * 4 + q, j // 2] = block[q * OUT : (q + 1) * OUT, :]
+            return carry
+
+        lax.fori_loop(0, 4, one, 0)
+
+    loads[4].wait()
+    for slot in (1, 2):
+        layer_copy(slot, 0).start()
+
     triangle = jnp.where(mask, 1.0, 0.0).astype(BF16)
     for b in range(2):
         sums[blocks[b], :] = dot_nn(triangle, features[blocks[b], :])
     zero = jnp.zeros((HEAD, 2 * HEAD), BF16)
-    for wave in range(YS):
-        for way in range(2):
-            for side in range(2):
-                zrecv[wave, way, side, 0] = zero
+    for v in range(ZFIRST):
+        for side in range(2):
+            zrecv[v, side, 0] = zero
     gstate[...] = jnp.zeros_like(gstate)
     gtotal[...] = jnp.zeros_like(gtotal)
     dkey[...] = jnp.zeros_like(dkey)
@@ -237,7 +274,11 @@
     loads[2].wait()
     lax.fori_loop(0, GROUP // 2, inside, 0)
     z_finish(0, states[0] + states[1], own_total, False)
+    for slot in (1, 2):
+        layer_copy(slot, 1).start()
     lax.fori_loop(GROUP // 2, GROUP, inside, 0)
+    turn(0, 0)
+    turn(0, 1)
     loads[3].wait()
     state, total = x_finish(0, False)
     for b in range(2):
@@ -251,141 +292,206 @@
     pack(message.at[1, 0], gstate[0] + gstate[1], own_gtotal)
     for k in range(1, ZS):
         z_copy(1, k).start()
+    for slot in (1, 2):
+        layer_copy(slot, 0).wait_recv()
+    layer_relay(0).start()
     lax.fori_loop(0, GROUP // 2, backward_pass, 0)
+    turn(1, 0)
+    turn(2, 0)
     z_finish(1, gstate[0] + gstate[1], own_gtotal, True)
     lax.fori_loop(GROUP // 2, GROUP, backward_pass, 0)
     grad_copy = pltpu.make_async_copy(grad_all, query_grad_hbm, load.at[5])
     grad_copy.start()
-    loads[4].wait()
-    for j in range(8):
-        block = layer[:, j * HEAD : (j + 1) * HEAD].T
-        for q in range(4):
-            turned[(j % 2) * 4 + q, j // 2] = block[q * OUT : (q + 1) * OUT, :]
+    for slot in (1, 2):
+        layer_copy(slot, 1).wait_recv()
+    layer_relay(1).start()
     later, later_total = x_finish(1, True)
     for b in (1, 0):
         later_high, later_low = halves(later)
         v = value[blocks[b], :]
         kf = features[blocks[b], :]
         dk = dkey[blocks[b], :] + dot_nt(v, later_high) + dot_nt(v, later_low) + later_total
-        gathered[0, core, blocks[b], 0:HEAD] = (dk * slope(key[blocks[b], :])).astype(BF16)
+        paired[core, blocks[b], 0:HEAD] = (dk * slope(key[blocks[b], :])).astype(BF16)
         dv = dvalue[blocks[b], :] + dot_nn(kf, later_high) + dot_nn(kf, later_low)
-        gathered[0, core, blocks[b], HEAD : 2 * HEAD] = dv.astype(BF16)
+        paired[core, blocks[b], HEAD : 2 * HEAD] = dv.astype(BF16)
         later = later + gstate[b]
         later_total = later_total + gtotal[b, 0:1, :]
 
-    def forward(slot):
+    swap = remote(paired.at[core], paired.at[core], f_send.at[0], f_recv.at[0], sibling)
+    swap_in = remote(paired.at[1 - core], paired.at[1 - core], f_send.at[0], f_recv.at[0], sibling)
+    swap.start()
+    swap_in.wait_recv()
+
+    def away_of(slot):
+        return slot + (slot // 2) * (1 - 2 * lax.rem(slot, 2))
+
+    def z_local(slot, way, to):
+        return dot_nn(turned[slot, to].reshape(XS * OUT, ROWS), paired[way])
+
+    def x_local(slot, way, to):
+        return dot_nn(turned[slot, :, to].reshape(ZS * OUT, ROWS), paired[way])
+
+    def z_hop(v, side, step):
+        sign = (1 - 2 * lax.rem(v, 2)) * (1 - 2 * side)
         return remote(
-            gathered.at[slot, core],
-            gathered.at[slot, core],
-            f_send.at[slot],
-            f_recv.at[slot],
-            sibling,
-        )
-
-    def forward_in(slot):
+            zsend.at[v, side, step],
+            zrecv.at[v, side, step + 1],
+            p_send.at[v, side, step],
+            p_recv.at[v, side, step + 1],
+            {"ctx": x * ZS + lax.rem(z + ZS + sign, ZS)},
+        )
+
+    def x_hop(u, kind):
+        sign = 1 - 2 * lax.rem(u, 2)
+        if kind == 2:
+            sign = -sign
         return remote(
-            gathered.at[slot, 1 - core],
-            gathered.at[slot, 1 - core],
-            f_send.at[slot],
-            f_recv.at[slot],
-            sibling,
-        )
-
-    def across(slot):
+            xsend.at[u, kind],
+            xrecv.at[u, kind],
+            q_send.at[u, kind],
+            q_recv.at[u, kind],
+            {"ctx": lax.rem(x + XS + sign, XS) * ZS + z},
+        )
+
+    def x_owe(v, k):
+        to = lax.rem(x + k, XS)
         return remote(
-            gathered.at[0, core],
-            gathered.at[slot, core],
-            y_send.at[slot],
-            y_recv.at[slot],
-            y_line[slot],
-        )
-
-    forward(0).start()
-    for slot in (1, 2, 3):
-        across(slot).start()
-
-    def hop(wave, way, side, step):
+            x_owed.at[v, to],
+            x_arrived.at[v, k],
+            x_send.at[v, k],
+            x_recv.at[v, k],
+            {"ctx": to * ZS + z, "head": lax.rem(y + away_of(v), YS) * 2 + core},
+        )
+
+    def z_owe(u, slot, k):
+        to = lax.rem(z + k, ZS)
         return remote(
-            zsend.at[wave, way, side, step],
-            zrecv.at[wave, way, side, step + 1],
-            p_send.at[wave, way, side, step],
-            p_recv.at[wave, way, side, step + 1],
-            z_line[1 if side == 0 else ZS - 1],
-        )
-
-    def owed(wave, k):
-        to = lax.rem(x + k, XS)
-        at = pl.ds(pl.multiple_of(to * OUT, OUT), OUT)
-        return remote(
-            reduced_low.at[wave, :, at, :],
-            arrived.at[wave, k],
-            x_send.at[wave, k],
-            x_recv.at[wave, k],
-            x_line[k],
-        )
-
-    def local(wave, way, to):
-        rows = turned[to].reshape(HEAD, ROWS)
-        return dot_nn(rows, gathered[wave, way])
+            z_owed.at[u, to],
+            z_arrived.at[u, k],
+            z_send.at[u, k],
+            z_recv.at[u, k],
+            {"ctx": x * ZS + to, "head": lax.rem(y + away_of(slot), YS) * 2 + core},
+        )
+
+    def z_first(v, step):
+        for side, hops in ((0, LONG), (1, SHORT)):
+
+            @pl.when((step >= 0) & (step < hops))
+            def _():
+                sign = (1 - 2 * lax.rem(v, 2)) * (1 - 2 * side)
+                to = lax.rem(z + ZS + sign * (hops - step), ZS)
+                mine = z_local(v, 0, to)
+
+                @pl.when(step > 0)
+                def _():
+                    z_hop(v, side, step - 1).wait_recv()
+
+                both = mine + zrecv[v, side, step].astype(F32)
+                zsend[v, side, step] = both.astype(BF16)
+                z_hop(v, side, step).start()
+
+        @pl.when(step == LONG)
+        def _():
+            total = z_local(v, 0, z)
+            z_hop(v, 0, LONG - 1).wait_recv()
+            z_hop(v, 1, SHORT - 1).wait_recv()
+            total = total + zrecv[v, 0, LONG].astype(F32) + zrecv[v, 1, SHORT].astype(F32)
+            x_owed[v] = total.astype(BF16).reshape(XS, OUT, 2 * HEAD)
+            for k in range(1, XS):
+                x_owe(v, k).start()
+
+            @pl.when(v == 0)
+            def _():
+                x_arrived[0, 0] = x_owed[0, x]
+
+            @pl.when(v > 0)
+            def _():
+                x_owe(v, 0).start()
+
+    def x_first(u, slot, way, step):
+        sign = 1 - 2 * lax.rem(u, 2)
+
+        @pl.when(step == 0)
+        def _():
+            xsend[u, 0] = x_local(slot, way, lax.rem(x + 2, XS)).astype(BF16)
+            x_hop(u, 0).start()
+            xsend[u, 2] = x_local(slot, way, lax.rem(x + XS - sign, XS)).astype(BF16)
+            x_hop(u, 2).start()
+
+        @pl.when(step == 1)
+        def _():
+            mine = x_local(slot, way, lax.rem(x + XS + sign, XS))
+            x_hop(u, 0).wait_recv()
+            xsend[u, 1] = (mine + xrecv[u, 0].astype(F32)).astype(BF16)
+            x_hop(u, 1).start()
+
+        @pl.when(step == 2)
+        def _():
+            total = x_local(slot, way, x)
+            x_hop(u, 1).wait_recv()
+            x_hop(u, 2).wait_recv()
+            total = total + xrecv[u, 1].astype(F32) + xrecv[u, 2].astype(F32)
+            z_owed[u] = total.astype(BF16).reshape(ZS, OUT, 2 * HEAD)
+
+            def one(k, carry):
+                z_owe(u, slot, k).start()
+                return carry
+
+            lax.fori_loop(1, ZS, one, 0)
+
+            @pl.when(slot == 0)
+            def _():
+                z_arrived[0, 0] = z_owed[0, z]
+
+            @pl.when(slot > 0)
+            def _():
+                z_owe(u, slot, 0).start()
 
     def tick(i, carry):
-        wave = lax.rem(i, YS)
-        step = i // YS - wave
-
-        for slot in range(1, YS):
-
-            @pl.when((step == -1) & (wave == slot))
-            def _():
-                across(slot).wait_recv()
-                forward(slot).start()
-
-        @pl.when(step == 0)
-        def _():
-            forward_in(wave).wait_recv()
-
+        slot = lax.rem(i, YS)
+        step = i // YS - slot
+
+        @pl.when((step == 0) & ((slot == 1) | (slot == 2)))
+        def _():
+            turn(slot, 1)
+
+        @pl.when((step == 0) & (slot == 3))
+        def _():
+            layer_relay(0).wait_recv()
+            turn(3, 0)
+            layer_relay(1).wait_recv()
+            turn(3, 1)
+
+        x_first(slot, slot, 1, step)
+
+        @pl.when(slot < ZFIRST)
+        def _():
+            z_first(slot, step)
+
+        @pl.when(slot == 3)
+        def _():
+            x_first(XFIRST - 1, 3, 0, step)
+
+        return carry
+
+    lax.fori_loop(0, YS * 7, tick, 0)
+    for slot in range(YS):
+        source = lax.rem(y + YS - (0, 1, 3, 2)[slot], YS) * 2
         for way in range(2):
-            for side in range(2):
-                hops = HOPS[way][side]
-
-                @pl.when((step >= 0) & (step < hops))
-                def _():
-                    left = hops - step
-                    to = lax.rem(z + left, ZS) if side == 0 else lax.rem(z + ZS - left, ZS)
-                    mine = local(wave, way, to)
-
-                    @pl.when(step > 0)
-                    def _():
-                        hop(wave, way, side, step - 1).wait_recv()
-
-                    both = mine + zrecv[wave, way, side, step].astype(F32)
-                    zsend[wave, way, side, step] = both.astype(BF16)
-                    hop(wave, way, side, step).start()
-
-        @pl.when(step == LAST)
-        def _():
-            for way in range(2):
-                total = local(wave, way, z)
-                for side in range(2):
-                    hops = HOPS[way][side]
-                    hop(wave, way, side, hops - 1).wait_recv()
-                    total = total + zrecv[wave, way, side, hops].astype(F32)
-                reduced[wave, way] = total
-                reduced_low[wave, way] = total.astype(BF16)
-            for k in range(1, XS):
-                owed(wave, k).start()
-
-        return carry
-
-    lax.fori_loop(0, YS * (LAST + YS), tick, 0)
-    mine_at = pl.ds(pl.multiple_of(x * OUT, OUT), OUT)
-    for wave in range(YS):
-        for k in range(1, XS):
-            owed(wave, k).wait_recv()
-        for way in range(2):
-            total = reduced[wave, way, mine_at, :]
-            for k in range(1, XS):
-                total = total + arrived[wave, k, way].astype(F32)
-            column = columns(lax.rem(y + away[wave], YS) * 2 + way)
+            first = 0 if slot else 1
+            if way == 0 and slot < ZFIRST:
+                for k in range(first, XS):
+                    x_owe(slot, k).wait_recv()
+                pieces = [x_arrived[slot, k] for k in range(XS)]
+            else:
+                u = slot if way else XFIRST - 1
+                for k in range(first, ZS):
+                    z_owe(u, slot, k).wait_recv()
+                pieces = [z_arrived[u, k] for k in range(ZS)]
+            total = pieces[0].astype(F32)
+            for piece in pieces[1:]:
+                total = total + piece.astype(F32)
+            column = columns(source + way)
             key_out[:, column] = total[:, 0:HEAD]
             value_out[:, column] = total[:, HEAD : 2 * HEAD]
 
@@ -394,21 +500,45 @@
             z_copy(e, k).wait_send()
         for k in range(1, XS):
             x_copy(e, k).wait_send()
-    forward(0).wait_send()
-    for slot in (1, 2, 3):
-        across(slot).wait_send()
-        forward(slot).wait_send()
-
-    def drain(wave, carry):
-        for way in range(2):
-            for side in range(2):
-                for step in range(HOPS[way][side]):
-                    hop(wave, way, side, step).wait_send()
+    for half in range(2):
+        for slot in (1, 2):
+            layer_copy(slot, half).wait_send()
+        layer_relay(half).wait_send()
+    swap.wait_send()
+
+    def drain_z(v, carry):
+        for side, hops in ((0, LONG), (1, SHORT)):
+            for step in range(hops):
+                z_hop(v, side, step).wait_send()
         for k in range(1, XS):
-            owed(wave, k).wait_send()
+            x_owe(v, k).wait_send()
+
+        @pl.when(v > 0)
+        def _():
+            x_owe(v, 0).wait_send()
+
         return carry
 
-    lax.fori_loop(0, YS, drain, 0)
+    lax.fori_loop(0, ZFIRST, drain_z, 0)
+
+    def drain_x(u, carry):
+        for kind in range(3):
+            x_hop(u, kind).wait_send()
+        slot = u - u // (XFIRST - 1)
+
+        def one(k, carry):
+            z_owe(u, slot, k).wait_send()
+            return carry
+
+        lax.fori_loop(1, ZS, one, 0)
+
+        @pl.when(u > 0)
+        def _():
+            z_owe(u, slot, 0).wait_send()
+
+        return carry
+
+    lax.fori_loop(0, XFIRST, drain_x, 0)
     grad_copy.wait()
 
 
@@ -433,7 +563,7 @@
             vmem((ROWS, wide), BF16),
             vmem((ROWS, HEAD), BF16),
             vmem((ROWS, HEAD), BF16),
-            vmem((ROWS, wide), BF16),
+            vmem((YS, ROWS, wide), BF16),
             vmem((ROWS, HEAD), BF16),
             vmem((ROWS, HEAD), F32),
             vmem((2, HEAD, HEAD), F32),
@@ -455,29 +585,36 @@
             vmem((2, 2, MESSAGE, HEAD), BF16),
             vmem((2, ZS, MESSAGE, HEAD), BF16),
             vmem((2, XS, MESSAGE, HEAD), BF16),
-            vmem((ZS, XS, OUT, ROWS), BF16),
-            vmem((YS, 2, ROWS, 2 * HEAD), BF16),
-            vmem((YS, 2, 2, LAST, HEAD, 2 * HEAD), BF16),
-            vmem((YS, 2, 2, LAST + 1, HEAD, 2 * HEAD), BF16),
-            vmem((YS, 2, HEAD, 2 * HEAD), F32),
-            vmem((YS, 2, HEAD, 2 * HEAD), BF16),
-            vmem((YS, XS, 2, OUT, 2 * HEAD), BF16),
+            vmem((YS, ZS, XS, OUT, ROWS), BF16),
+            vmem((2, ROWS, 2 * HEAD), BF16),
+            vmem((ZFIRST, 2, LONG, XS * OUT, 2 * HEAD), BF16),
+            vmem((ZFIRST, 2, LONG + 1, XS * OUT, 2 * HEAD), BF16),
+            vmem((XFIRST, 3, ZS * OUT, 2 * HEAD), BF16),
+            vmem((XFIRST, 3, ZS * OUT, 2 * HEAD), BF16),
+            vmem((ZFIRST, XS, OUT, 2 * HEAD), BF16),
+            vmem((XFIRST, ZS, OUT, 2 * HEAD), BF16),
+            vmem((ZFIRST, XS, OUT, 2 * HEAD), BF16),
+            vmem((XFIRST, ZS, OUT, 2 * HEAD), BF16),
             sems((6,)),
             sems((2, ZS)),
             sems((2, ZS)),
             sems((2, XS)),
             sems((2, XS)),
-            sems((YS,)),
-            sems((YS,)),
-            sems((YS,)),
-            sems((YS,)),
-            sems((YS, 2, 2, LAST)),
-            sems((YS, 2, 2, LAST + 1)),
-            sems((YS, XS)),
-            sems((YS, XS)),
+            sems((YS, 2)),
+            sems((YS, 2)),
+            sems((1,)),
+            sems((1,)),
+            sems((ZFIRST, 2, LONG)),
+            sems((ZFIRST, 2, LONG + 1)),
+            sems((XFIRST, 3)),
+            sems((XFIRST, 3)),
+            sems((ZFIRST, XS)),
+            sems((ZFIRST, XS)),
+            sems((XFIRST, ZS)),
+            sems((XFIRST, ZS)),
         ],
         compiler_params=pltpu.CompilerParams(
-            collective_id=0, has_side_effects=True, vmem_limit_bytes=48 << 20
+            collective_id=0, has_side_effects=True, vmem_limit_bytes=LIMIT
         ),
         name="backward",
     )(query_columns, output_gradient, key_columns, value_columns, layer_input)

time: 102 us -> 91 us (0.89); the launches traced: 101 us -> 90.8 us
  Pallas kernels: 92.3 us -> 86.3 us
  local copies, waits for them, and re-layouts: 7.76 us -> 3.91 us
    pallas_call x1, Pallas kernels: 92.3 us -> 86.3 us  [shards(): pl.pallas_call(kernel, out_shape=(shape((ROWS, wide), BF16), shape((OUT,...]
    unnamed x13 -> x7, local copies, waits for them, and re-layouts: 7.76 us -> 3.91 us
where the time goes in v3:
time: 91 us; the launch traced here: 90.8 us
  Pallas kernels  86.3 us (95%)
  local copies, waits for them, and re-layouts  3.91 us (4%)
    pallas_call x1, Pallas kernels, shards(): pl.pallas_call(kernel, out_shape=(shape((ROWS, wide), BF16), shape((OUT,...  86.3 us
    unnamed x7, local copies, waits for them, and re-layouts  3.91 us

profile of v3, /device:TPU:8, one launch (start us, length us, event | category | flops | bytes accessed | tf_op | source)
XLA Modules:
  0.0 90.8 jit_solution(17784906203548322450)
XLA Ops:
  0.6 86.3 %backward.1 = (bf16[512,1024]{1,0:T(8,128)(2,1)}, f32[32,1024]{1,0:T(8,128)}, f32[32,1024]{1,0:T(8,128)}) custom-call(bf16[512,1024]{1,0:T(8,128)(2,1)} %query_hbm.1, bf16[512,1024]{1,0:T(8,128)(2,1)} %cotangent_hbm.1, bf16[512,128]{1,0:T(8,128)(2,1)} %key_hbm.1, bf16[512,128]{1,0:T(8,128)(2,1)} %value_hbm.1, bf16[512,1024]{1,0:T(8,128)(2,1)} %layer_hbm.1), custom_call_target="tpu_custom_call" | custom-call | tf_op jit(solution)/shard_map/backward/pallas_call | solution.py:552
  86.9 0.0 copy-start.1
  86.9 2.3 %copy.11 = bf16[512,1024]{1,0:T(8,128)(2,1)} copy(bf16[512,1024]{1,0:T(8,128)(2,1)} %get-tuple-element.6) | data formatting | bytes 2097152
  89.2 0.0 copy-done.1
  89.2 0.0 copy-start
  89.2 0.7 copy.12
  89.9 0.3 copy-done
  90.2 0.7 copy.13
Async XLA Ops:
  86.9 2.3 %copy-start.1 = (f32[32,1024]{1,0:T(8,128)S(1)}, f32[32,1024]{1,0:T(8,128)}, u32[]{:S(2)}) copy-start(f32[32,1024]{1,0:T(8,128)} %get-tuple-element.7) | copy-start | bytes 393220
  89.2 1.0 %copy-start = (f32[32,1024]{1,0:T(8,128)S(1)}, f32[32,1024]{1,0:T(8,128)}, u32[]{:S(2)}) copy-start(f32[32,1024]{1,0:T(8,128)} %get-tuple-element.8) | copy-start | bytes 393220

commit v4 on v3

--- a/solution.py
+++ b/solution.py
@@ -22,8 +22,34 @@
 HALF = 512
 LONG = 4
 SHORT = 3
-ZFIRST = 3
-XFIRST = 5
+NEAR = 5
+ORDER = (
+    ("x", 0, 0, 1),
+    ("z", 0, 0, 1),
+    ("turn", 1, 0, 0),
+    ("x", 0, 1, 2),
+    ("z", 0, 1, 2),
+    ("turn", 2, 0, 0),
+    ("x", 0, 2, 3),
+    ("z", 0, 2, 3),
+    ("z", 1, 0, 3),
+    ("x", 1, 0, 3),
+    ("turn", 3, 0, 0),
+    ("z", 0, 3, 4),
+    ("x", 0, 3, 4),
+    ("z", 2, 0, 3),
+    ("x", 2, 0, 3),
+    ("z", 1, 3, 4),
+    ("x", 1, 3, 4),
+    ("z", 3, 0, 3),
+    ("x", 3, 0, 3),
+    ("z", 2, 3, 4),
+    ("x", 2, 3, 4),
+    ("z", 4, 0, 3),
+    ("z", 3, 3, 4),
+    ("x", 3, 3, 4),
+    ("z", 4, 3, 4),
+)
 LIMIT = 60 << 20
 
 
@@ -91,9 +117,9 @@
     qf_all, scores_all, numer_all, g_all, c_all, grad_all,
     gstate, gtotal, dkey, dvalue,
     message, from_z, from_x,
-    turned, paired, zsend, zrecv, xsend, xrecv, x_owed, z_owed, x_arrived, z_arrived,
+    turned, paired, zsend, zrecv, xsend, xrecv, x_owed, z_owed, x_arrived, z_arrived, z_passed, z_joined,
     load, zs, zr, xs, xr, l_send, l_recv, f_send, f_recv,
-    p_send, p_recv, q_send, q_recv, x_send, x_recv, z_send, z_recv,
+    p_send, p_recv, q_send, q_recv, x_send, x_recv, z_send, z_recv, m_send, m_recv,
 ):
     me = lax.axis_index("ctx")
     head = lax.axis_index("head")
@@ -211,10 +237,6 @@
     triangle = jnp.where(mask, 1.0, 0.0).astype(BF16)
     for b in range(2):
         sums[blocks[b], :] = dot_nn(triangle, features[blocks[b], :])
-    zero = jnp.zeros((HEAD, 2 * HEAD), BF16)
-    for v in range(ZFIRST):
-        for side in range(2):
-            zrecv[v, side, 0] = zero
     gstate[...] = jnp.zeros_like(gstate)
     gtotal[...] = jnp.zeros_like(gtotal)
     dkey[...] = jnp.zeros_like(dkey)
@@ -363,138 +385,131 @@
             {"ctx": to * ZS + z, "head": lax.rem(y + away_of(v), YS) * 2 + core},
         )
 
-    def z_owe(u, slot, k):
-        to = lax.rem(z + k, ZS)
+    def z_at(k):
+        return lax.rem(z + ZS + k, ZS)
+
+    def z_owe(u, kind):
+        if kind < 3:
+            to = z_at((0, 1, -1)[kind])
+            source = z_owed.at[u, to]
+        else:
+            to = z_at((2, -2)[kind - 3])
+            source = z_joined.at[u, kind - 3]
         return remote(
-            z_owed.at[u, to],
-            z_arrived.at[u, k],
-            z_send.at[u, k],
-            z_recv.at[u, k],
-            {"ctx": x * ZS + to, "head": lax.rem(y + away_of(slot), YS) * 2 + core},
-        )
-
-    def z_first(v, step):
-        for side, hops in ((0, LONG), (1, SHORT)):
-
-            @pl.when((step >= 0) & (step < hops))
-            def _():
+            source,
+            z_arrived.at[u, kind],
+            z_send.at[u, kind],
+            z_recv.at[u, kind],
+            {"ctx": x * ZS + to, "head": lax.rem(y + away_of(u), YS) * 2 + core},
+        )
+
+    def z_pass(u, kind):
+        sign = 1 - 2 * lax.rem(u, 2)
+        chunk = z_at((3, -3, 4)[kind])
+        to = z_at((1, -1, 2 * sign)[kind])
+        return remote(
+            z_owed.at[u, chunk],
+            z_passed.at[u, kind],
+            m_send.at[u, kind],
+            m_recv.at[u, kind],
+            {"ctx": x * ZS + to},
+        )
+
+    def z_step(step):
+        def run(v, carry):
+            if step == LONG:
+                total = z_local(v, 0, z)
+                z_hop(v, 0, LONG - 1).wait_recv()
+                z_hop(v, 1, SHORT - 1).wait_recv()
+                total = total + zrecv[v, 0, LONG].astype(F32) + zrecv[v, 1, SHORT].astype(F32)
+                x_owed[v] = total.astype(BF16).reshape(XS, OUT, 2 * HEAD)
+                for k in range(1, XS):
+                    x_owe(v, k).start()
+
+                @pl.when(v == 0)
+                def _():
+                    x_arrived[0, 0] = x_owed[0, x]
+
+                @pl.when(v > 0)
+                def _():
+                    x_owe(v, 0).start()
+
+                return carry
+            for side, hops in ((0, LONG), (1, SHORT)):
+                if step >= hops:
+                    continue
                 sign = (1 - 2 * lax.rem(v, 2)) * (1 - 2 * side)
                 to = lax.rem(z + ZS + sign * (hops - step), ZS)
-                mine = z_local(v, 0, to)
-
-                @pl.when(step > 0)
-                def _():
+                both = z_local(v, 0, to)
+                if step > 0:
                     z_hop(v, side, step - 1).wait_recv()
-
-                both = mine + zrecv[v, side, step].astype(F32)
+                    both = both + zrecv[v, side, step].astype(F32)
                 zsend[v, side, step] = both.astype(BF16)
                 z_hop(v, side, step).start()
-
-        @pl.when(step == LONG)
-        def _():
-            total = z_local(v, 0, z)
-            z_hop(v, 0, LONG - 1).wait_recv()
-            z_hop(v, 1, SHORT - 1).wait_recv()
-            total = total + zrecv[v, 0, LONG].astype(F32) + zrecv[v, 1, SHORT].astype(F32)
-            x_owed[v] = total.astype(BF16).reshape(XS, OUT, 2 * HEAD)
-            for k in range(1, XS):
-                x_owe(v, k).start()
-
-            @pl.when(v == 0)
-            def _():
-                x_arrived[0, 0] = x_owed[0, x]
-
-            @pl.when(v > 0)
-            def _():
-                x_owe(v, 0).start()
-
-    def x_first(u, slot, way, step):
-        sign = 1 - 2 * lax.rem(u, 2)
-
-        @pl.when(step == 0)
-        def _():
-            xsend[u, 0] = x_local(slot, way, lax.rem(x + 2, XS)).astype(BF16)
-            x_hop(u, 0).start()
-            xsend[u, 2] = x_local(slot, way, lax.rem(x + XS - sign, XS)).astype(BF16)
-            x_hop(u, 2).start()
-
-        @pl.when(step == 1)
-        def _():
-            mine = x_local(slot, way, lax.rem(x + XS + sign, XS))
-            x_hop(u, 0).wait_recv()
-            xsend[u, 1] = (mine + xrecv[u, 0].astype(F32)).astype(BF16)
-            x_hop(u, 1).start()
-
-        @pl.when(step == 2)
-        def _():
+            return carry
+
+        return run
+
+    def x_step(step):
+        def run(u, carry):
+            slot, way = u, 1
+            sign = 1 - 2 * lax.rem(u, 2)
+            if step == 0:
+                xsend[u, 0] = x_local(slot, way, lax.rem(x + 2, XS)).astype(BF16)
+                x_hop(u, 0).start()
+                xsend[u, 2] = x_local(slot, way, lax.rem(x + XS - sign, XS)).astype(BF16)
+                x_hop(u, 2).start()
+                return carry
+            if step == 1:
+                mine = x_local(slot, way, lax.rem(x + XS + sign, XS))
+                x_hop(u, 0).wait_recv()
+                xsend[u, 1] = (mine + xrecv[u, 0].astype(F32)).astype(BF16)
+                x_hop(u, 1).start()
+                return carry
+            if step == 3:
+                for kind in range(3):
+                    z_pass(u, kind).wait_recv()
+                extra = z_passed[u, 2].astype(F32)
+                for side in range(2):
+                    total = z_owed[u, z_at((2, -2)[side])].astype(F32)
+                    total = total + z_passed[u, side].astype(F32)
+                    total = total + jnp.where(lax.rem(u, 2) == side, extra, 0.0)
+                    z_joined[u, side] = total.astype(BF16)
+                    z_owe(u, 3 + side).start()
+                return carry
             total = x_local(slot, way, x)
             x_hop(u, 1).wait_recv()
             x_hop(u, 2).wait_recv()
             total = total + xrecv[u, 1].astype(F32) + xrecv[u, 2].astype(F32)
             z_owed[u] = total.astype(BF16).reshape(ZS, OUT, 2 * HEAD)
-
-            def one(k, carry):
-                z_owe(u, slot, k).start()
-                return carry
-
-            lax.fori_loop(1, ZS, one, 0)
-
-            @pl.when(slot == 0)
+            for kind in (2, 0, 1):
+                z_pass(u, kind).start()
+            for kind in (1, 2):
+                z_owe(u, kind).start()
+
+            @pl.when(u == 0)
             def _():
                 z_arrived[0, 0] = z_owed[0, z]
 
-            @pl.when(slot > 0)
+            @pl.when(u > 0)
             def _():
-                z_owe(u, slot, 0).start()
-
-    def tick(i, carry):
-        slot = lax.rem(i, YS)
-        step = i // YS - slot
-
-        @pl.when((step == 0) & ((slot == 1) | (slot == 2)))
-        def _():
-            turn(slot, 1)
-
-        @pl.when((step == 0) & (slot == 3))
-        def _():
-            layer_relay(0).wait_recv()
-            turn(3, 0)
-            layer_relay(1).wait_recv()
-            turn(3, 1)
-
-        x_first(slot, slot, 1, step)
-
-        @pl.when(slot < ZFIRST)
-        def _():
-            z_first(slot, step)
-
-        @pl.when(slot == 3)
-        def _():
-            x_first(XFIRST - 1, 3, 0, step)
-
-        return carry
-
-    lax.fori_loop(0, YS * 7, tick, 0)
-    for slot in range(YS):
-        source = lax.rem(y + YS - (0, 1, 3, 2)[slot], YS) * 2
-        for way in range(2):
-            first = 0 if slot else 1
-            if way == 0 and slot < ZFIRST:
-                for k in range(first, XS):
-                    x_owe(slot, k).wait_recv()
-                pieces = [x_arrived[slot, k] for k in range(XS)]
-            else:
-                u = slot if way else XFIRST - 1
-                for k in range(first, ZS):
-                    z_owe(u, slot, k).wait_recv()
-                pieces = [z_arrived[u, k] for k in range(ZS)]
-            total = pieces[0].astype(F32)
-            for piece in pieces[1:]:
-                total = total + piece.astype(F32)
-            column = columns(source + way)
-            key_out[:, column] = total[:, 0:HEAD]
-            value_out[:, column] = total[:, HEAD : 2 * HEAD]
-
+                z_owe(u, 0).start()
+
+            return carry
+
+        return run
+
+    for kind, step, first, end in ORDER:
+        if kind == "x":
+            lax.fori_loop(first, end, x_step(step), 0)
+        elif kind == "z":
+            lax.fori_loop(first, end, z_step(step), 0)
+        else:
+            if step == 3:
+                layer_relay(0).wait_recv()
+                turn(3, 0)
+                layer_relay(1).wait_recv()
+            turn(step, 1)
     for e in range(2):
         for k in range(1, ZS):
             z_copy(e, k).wait_send()
@@ -506,40 +521,50 @@
         layer_relay(half).wait_send()
     swap.wait_send()
 
-    def drain_z(v, carry):
+    def drain(u, carry):
         for side, hops in ((0, LONG), (1, SHORT)):
             for step in range(hops):
-                z_hop(v, side, step).wait_send()
-        for k in range(1, XS):
-            x_owe(v, k).wait_send()
-
-        @pl.when(v > 0)
-        def _():
-            x_owe(v, 0).wait_send()
-
-        return carry
-
-    lax.fori_loop(0, ZFIRST, drain_z, 0)
-
-    def drain_x(u, carry):
+                z_hop(u, side, step).wait_send()
         for kind in range(3):
             x_hop(u, kind).wait_send()
-        slot = u - u // (XFIRST - 1)
-
-        def one(k, carry):
-            z_owe(u, slot, k).wait_send()
-            return carry
-
-        lax.fori_loop(1, ZS, one, 0)
+            z_pass(u, kind).wait_send()
+        return carry
+
+    lax.fori_loop(0, YS, drain, 0)
+    grad_copy.wait()
+    for slot in range(YS):
+        source = lax.rem(y + YS - (0, 1, 3, 2)[slot], YS) * 2
+        for way in range(2):
+            first = 0 if slot else 1
+            if way == 0:
+                for k in range(first, XS):
+                    x_owe(slot, k).wait_recv()
+                pieces = [x_arrived[slot, k] for k in range(XS)]
+            else:
+                for kind in range(first, NEAR):
+                    z_owe(slot, kind).wait_recv()
+                pieces = [z_arrived[slot, kind] for kind in range(NEAR)]
+            total = pieces[0].astype(F32)
+            for piece in pieces[1:]:
+                total = total + piece.astype(F32)
+            column = columns(source + way)
+            key_out[:, column] = total[:, 0:HEAD]
+            value_out[:, column] = total[:, HEAD : 2 * HEAD]
+
+    def drain_last(u, carry):
+        for k in range(1, XS):
+            x_owe(u, k).wait_send()
+        for kind in range(1, NEAR):
+            z_owe(u, kind).wait_send()
 
         @pl.when(u > 0)
         def _():
-            z_owe(u, slot, 0).wait_send()
+            x_owe(u, 0).wait_send()
+            z_owe(u, 0).wait_send()
 
         return carry
 
-    lax.fori_loop(0, XFIRST, drain_x, 0)
-    grad_copy.wait()
+    lax.fori_loop(0, YS, drain_last, 0)
 
 
 def shards(layer_input, query_columns, key_columns, value_columns, output_gradient):
@@ -587,14 +612,16 @@
             vmem((2, XS, MESSAGE, HEAD), BF16),
             vmem((YS, ZS, XS, OUT, ROWS), BF16),
             vmem((2, ROWS, 2 * HEAD), BF16),
-            vmem((ZFIRST, 2, LONG, XS * OUT, 2 * HEAD), BF16),
-            vmem((ZFIRST, 2, LONG + 1, XS * OUT, 2 * HEAD), BF16),
-            vmem((XFIRST, 3, ZS * OUT, 2 * HEAD), BF16),
-            vmem((XFIRST, 3, ZS * OUT, 2 * HEAD), BF16),
-            vmem((ZFIRST, XS, OUT, 2 * HEAD), BF16),
-            vmem((XFIRST, ZS, OUT, 2 * HEAD), BF16),
-            vmem((ZFIRST, XS, OUT, 2 * HEAD), BF16),
-            vmem((XFIRST, ZS, OUT, 2 * HEAD), BF16),
+            vmem((YS, 2, LONG, XS * OUT, 2 * HEAD), BF16),
+            vmem((YS, 2, LONG + 1, XS * OUT, 2 * HEAD), BF16),
+            vmem((YS, 3, ZS * OUT, 2 * HEAD), BF16),
+            vmem((YS, 3, ZS * OUT, 2 * HEAD), BF16),
+            vmem((YS, XS, OUT, 2 * HEAD), BF16),
+            vmem((YS, ZS, OUT, 2 * HEAD), BF16),
+            vmem((YS, XS, OUT, 2 * HEAD), BF16),
+            vmem((YS, NEAR, OUT, 2 * HEAD), BF16),
+            vmem((YS, 3, OUT, 2 * HEAD), BF16),
+            vmem((YS, 2, OUT, 2 * HEAD), BF16),
             sems((6,)),
             sems((2, ZS)),
             sems((2, ZS)),
@@ -604,14 +631,16 @@
             sems((YS, 2)),
             sems((1,)),
             sems((1,)),
-            sems((ZFIRST, 2, LONG)),
-            sems((ZFIRST, 2, LONG + 1)),
-            sems((XFIRST, 3)),
-            sems((XFIRST, 3)),
-            sems((ZFIRST, XS)),
-            sems((ZFIRST, XS)),
-            sems((XFIRST, ZS)),
-            sems((XFIRST, ZS)),
+            sems((YS, 2, LONG)),
+            sems((YS, 2, LONG + 1)),
+            sems((YS, 3)),
+            sems((YS, 3)),
+            sems((YS, XS)),
+            sems((YS, XS)),
+            sems((YS, NEAR)),
+            sems((YS, NEAR)),
+            sems((YS, 3)),
+            sems((YS, 3)),
         ],
         compiler_params=pltpu.CompilerParams(
             collective_id=0, has_side_effects=True, vmem_limit_bytes=LIMIT

time: 91 us -> 85.7 us (0.942)
  the two profiles are of different devices: /device:TPU:8 before, /device:TPU:1 now
where the time goes in v4:
time: 85.7 us; the launch traced here: 85.6 us
  Pallas kernels  81 us (95%)
  local copies, waits for them, and re-layouts  3.91 us (5%)
    pallas_call x1, Pallas kernels, shards(): pl.pallas_call(kernel, out_shape=(shape((ROWS, wide), BF16), shape((OUT,...  81 us
    unnamed x7, local copies, waits for them, and re-layouts  3.91 us

profile of v4, /device:TPU:1, one launch (start us, length us, event | category | flops | bytes accessed | tf_op | source)
XLA Modules:
  0.0 85.6 jit_solution(18439638832345147621)
XLA Ops:
  0.6 81.0 %backward.1 = (bf16[512,1024]{1,0:T(8,128)(2,1)}, f32[32,1024]{1,0:T(8,128)}, f32[32,1024]{1,0:T(8,128)}) custom-call(bf16[512,1024]{1,0:T(8,128)(2,1)} %query_hbm.1, bf16[512,1024]{1,0:T(8,128)(2,1)} %cotangent_hbm.1, bf16[512,128]{1,0:T(8,128)(2,1)} %key_hbm.1, bf16[512,128]{1,0:T(8,128)(2,1)} %value_hbm.1, bf16[512,1024]{1,0:T(8,128)(2,1)} %layer_hbm.1), custom_call_target="tpu_custom_call" | custom-call | tf_op jit(solution)/shard_map/backward/pallas_call | solution.py:577
  81.7 0.0 copy-start.1
  81.7 2.3 %copy.11 = bf16[512,1024]{1,0:T(8,128)(2,1)} copy(bf16[512,1024]{1,0:T(8,128)(2,1)} %get-tuple-element.6) | data formatting | bytes 2097152
  84.0 0.0 copy-done.1
  84.0 0.0 copy-start
  84.0 0.7 copy.12
  84.7 0.3 copy-done
  84.9 0.7 copy.13
Async XLA Ops:
  81.7 2.3 %copy-start.1 = (f32[32,1024]{1,0:T(8,128)S(1)}, f32[32,1024]{1,0:T(8,128)}, u32[]{:S(2)}) copy-start(f32[32,1024]{1,0:T(8,128)} %get-tuple-element.7) | copy-start | bytes 393220
  84.0 1.0 %copy-start = (f32[32,1024]{1,0:T(8,128)S(1)}, f32[32,1024]{1,0:T(8,128)}, u32[]{:S(2)}) copy-start(f32[32,1024]{1,0:T(8,128)} %get-tuple-element.8) | copy-start | bytes 393220

commit v5 on v4

--- a/solution.py
+++ b/solution.py
@@ -26,31 +26,32 @@
 ORDER = (
     ("x", 0, 0, 1),
     ("z", 0, 0, 1),
-    ("turn", 1, 0, 0),
     ("x", 0, 1, 2),
     ("z", 0, 1, 2),
-    ("turn", 2, 0, 0),
     ("x", 0, 2, 3),
     ("z", 0, 2, 3),
+    ("turn", 0, 0, 0),
     ("z", 1, 0, 3),
-    ("x", 1, 0, 3),
-    ("turn", 3, 0, 0),
+    ("x", 1, 0, 2),
+    ("turn", 1, 0, 0),
     ("z", 0, 3, 4),
     ("x", 0, 3, 4),
+    ("x", 1, 2, 3),
     ("z", 2, 0, 3),
+    ("z", 1, 3, 4),
     ("x", 2, 0, 3),
-    ("z", 1, 3, 4),
     ("x", 1, 3, 4),
     ("z", 3, 0, 3),
+    ("z", 2, 3, 4),
     ("x", 3, 0, 3),
-    ("z", 2, 3, 4),
     ("x", 2, 3, 4),
     ("z", 4, 0, 3),
     ("z", 3, 3, 4),
     ("x", 3, 3, 4),
     ("z", 4, 3, 4),
 )
-LIMIT = 60 << 20
+EARLY = 6
+LIMIT = 52 << 20
 
 
 def phi(raw):
@@ -144,11 +145,13 @@
             )
         )
     ]
-    for copy in loads:
-        copy.start()
+    loads[0].start()
+    loads[1].start()
     barrier = pltpu.get_barrier_semaphore()
     for device in z_line[1:] + x_line[1:] + y_line[1:] + [sibling]:
         pl.semaphore_signal(barrier, inc=1, device_id=device, device_id_type=MESH)
+    for copy in loads[2:]:
+        copy.start()
 
     def z_copy(e, k):
         return remote(message.at[e, 0], from_z.at[e, k], zs.at[e, k], zr.at[e, k], z_line[k])
@@ -317,16 +320,18 @@
     for slot in (1, 2):
         layer_copy(slot, 0).wait_recv()
     layer_relay(0).start()
-    lax.fori_loop(0, GROUP // 2, backward_pass, 0)
+    lax.fori_loop(0, EARLY, backward_pass, 0)
     turn(1, 0)
     turn(2, 0)
     z_finish(1, gstate[0] + gstate[1], own_gtotal, True)
-    lax.fori_loop(GROUP // 2, GROUP, backward_pass, 0)
+    lax.fori_loop(EARLY, GROUP, backward_pass, 0)
     grad_copy = pltpu.make_async_copy(grad_all, query_grad_hbm, load.at[5])
     grad_copy.start()
     for slot in (1, 2):
         layer_copy(slot, 1).wait_recv()
     layer_relay(1).start()
+    turn(1, 1)
+    turn(2, 1)
     later, later_total = x_finish(1, True)
     for b in (1, 0):
         later_high, later_low = halves(later)
@@ -505,11 +510,8 @@
         elif kind == "z":
             lax.fori_loop(first, end, z_step(step), 0)
         else:
-            if step == 3:
-                layer_relay(0).wait_recv()
-                turn(3, 0)
-                layer_relay(1).wait_recv()
-            turn(step, 1)
+            layer_relay(step).wait_recv()
+            turn(3, step)
     for e in range(2):
         for k in range(1, ZS):
             z_copy(e, k).wait_send()

time: 85.7 us -> 83 us (0.968)
  the two profiles are of different devices: /device:TPU:1 before, /device:TPU:8 now
where the time goes in v5:
time: 83 us; the launch traced here: 81.4 us
  Pallas kernels  76.6 us (92%)
  local copies, waits for them, and re-layouts  4.08 us (5%)
    pallas_call x1, Pallas kernels, shards(): pl.pallas_call(kernel, out_shape=(shape((ROWS, wide), BF16), shape((OUT,...  76.6 us
    unnamed x7, local copies, waits for them, and re-layouts  4.08 us

profile of v5, /device:TPU:8, one launch (start us, length us, event | category | flops | bytes accessed | tf_op | source)
XLA Modules:
  0.0 81.4 jit_solution(9915741188340462550)
XLA Ops:
  0.6 0.0 copy-start
  0.6 0.9 %copy-done = bf16[512,128]{1,0:T(8,128)(2,1)S(1)} copy-done((bf16[512,128]{1,0:T(8,128)(2,1)S(1)}, bf16[512,128]{1,0:T(8,128)(2,1)}, u32[]{:S(2)}) %copy-start) | copy-done | bytes 131096
  1.5 0.0 copy-start.1
  1.5 0.9 %copy-done.1 = bf16[512,128]{1,0:T(8,128)(2,1)S(1)} copy-done((bf16[512,128]{1,0:T(8,128)(2,1)S(1)}, bf16[512,128]{1,0:T(8,128)(2,1)}, u32[]{:S(2)}) %copy-start.1) | copy-done | bytes 131096
  2.4 76.6 %backward.1 = (bf16[512,1024]{1,0:T(8,128)(2,1)S(1)}, f32[32,1024]{1,0:T(8,128)S(1)}, f32[32,1024]{1,0:T(8,128)S(1)}) custom-call(bf16[512,1024]{1,0:T(8,128)(2,1)} %query_hbm.1, bf16[512,1024]{1,0:T(8,128)(2,1)} %cotangent_hbm.1, bf16[512,128]{1,0:T(8,128)(2,1)S(1)} %copy-done, bf16[512,128]{1,0:T(8,128)(2,1)S(1)} %copy-done.1, bf16[512,1024]{1,0:T(8,128)(2,1)} %layer_hbm.1), custom_call_target="tpu_custom_call" | custom-call | tf_op jit(solution)/shard_map/backward/pallas_call | solution.py:579
  79.1 1.0 %copy.11 = bf16[512,1024]{1,0:T(8,128)(2,1)} copy(bf16[512,1024]{1,0:T(8,128)(2,1)S(1)} %get-tuple-element.6) | data formatting | bytes 2097152
  80.0 0.7 copy.12
  80.7 0.7 copy.13
Async XLA Ops:
  0.6 0.9 %copy-start = (bf16[512,128]{1,0:T(8,128)(2,1)S(1)}, bf16[512,128]{1,0:T(8,128)(2,1)}, u32[]{:S(2)}) copy-start(bf16[512,128]{1,0:T(8,128)(2,1)} %key_hbm.1) | copy-start | bytes 393220
  1.5 0.9 %copy-start.1 = (bf16[512,128]{1,0:T(8,128)(2,1)S(1)}, bf16[512,128]{1,0:T(8,128)(2,1)}, u32[]{:S(2)}) copy-start(bf16[512,128]{1,0:T(8,128)(2,1)} %value_hbm.1) | copy-start | bytes 393220

commit v6 on v5

--- a/solution.py
+++ b/solution.py
@@ -312,7 +312,7 @@
         sums[blocks[b], :] += total
         state = state + states[b]
         total = total + totals[b, 0:1, :]
-    lax.fori_loop(0, GROUP, forward_pass, 0)
+    lax.fori_loop(0, GROUP, forward_pass, 0, unroll=2)
     own_gtotal = gtotal[0, 0:1, :] + gtotal[1, 0:1, :]
     pack(message.at[1, 0], gstate[0] + gstate[1], own_gtotal)
     for k in range(1, ZS):

time: 83 us -> 81.9 us (0.987)
  Pallas kernels: 76.6 us -> 75.6 us
    pallas_call x1, Pallas kernels: 76.6 us -> 75.6 us  [shards(): pl.pallas_call(kernel, out_shape=(shape((ROWS, wide), BF16), shape((OUT,...]
where the time goes in v6:
time: 81.9 us; the launch traced here: 80.3 us
  Pallas kernels  75.6 us (92%)
  local copies, waits for them, and re-layouts  4.08 us (5%)
    pallas_call x1, Pallas kernels, shards(): pl.pallas_call(kernel, out_shape=(shape((ROWS, wide), BF16), shape((OUT,...  75.6 us
    unnamed x7, local copies, waits for them, and re-layouts  4.08 us

profile of v6, /device:TPU:8, one launch (start us, length us, event | category | flops | bytes accessed | tf_op | source)
XLA Modules:
  0.0 80.3 jit_solution(5681158925884084413)
XLA Ops:
  0.6 0.0 copy-start
  0.6 0.9 %copy-done = bf16[512,128]{1,0:T(8,128)(2,1)S(1)} copy-done((bf16[512,128]{1,0:T(8,128)(2,1)S(1)}, bf16[512,128]{1,0:T(8,128)(2,1)}, u32[]{:S(2)}) %copy-start) | copy-done | bytes 131096
  1.5 0.0 copy-start.1
  1.5 0.9 %copy-done.1 = bf16[512,128]{1,0:T(8,128)(2,1)S(1)} copy-done((bf16[512,128]{1,0:T(8,128)(2,1)S(1)}, bf16[512,128]{1,0:T(8,128)(2,1)}, u32[]{:S(2)}) %copy-start.1) | copy-done | bytes 131096
  2.4 75.6 %backward.1 = (bf16[512,1024]{1,0:T(8,128)(2,1)S(1)}, f32[32,1024]{1,0:T(8,128)S(1)}, f32[32,1024]{1,0:T(8,128)S(1)}) custom-call(bf16[512,1024]{1,0:T(8,128)(2,1)} %query_hbm.1, bf16[512,1024]{1,0:T(8,128)(2,1)} %cotangent_hbm.1, bf16[512,128]{1,0:T(8,128)(2,1)S(1)} %copy-done, bf16[512,128]{1,0:T(8,128)(2,1)S(1)} %copy-done.1, bf16[512,1024]{1,0:T(8,128)(2,1)} %layer_hbm.1), custom_call_target="tpu_custom_call" | custom-call | tf_op jit(solution)/shard_map/backward/pallas_call | solution.py:579
  78.0 1.0 %copy.11 = bf16[512,1024]{1,0:T(8,128)(2,1)} copy(bf16[512,1024]{1,0:T(8,128)(2,1)S(1)} %get-tuple-element.6) | data formatting | bytes 2097152
  79.0 0.7 copy.12
  79.7 0.7 copy.13
Async XLA Ops:
  0.6 0.9 %copy-start = (bf16[512,128]{1,0:T(8,128)(2,1)S(1)}, bf16[512,128]{1,0:T(8,128)(2,1)}, u32[]{:S(2)}) copy-start(bf16[512,128]{1,0:T(8,128)(2,1)} %key_hbm.1) | copy-start | bytes 393220
  1.5 0.9 %copy-start.1 = (bf16[512,128]{1,0:T(8,128)(2,1)S(1)}, bf16[512,128]{1,0:T(8,128)(2,1)}, u32[]{:S(2)}) copy-start(bf16[512,128]{1,0:T(8,128)(2,1)} %value_hbm.1) | copy-start | bytes 393220
